TPU v7x, 128 devices: a whole 4x4x4 slice. The times are simulated.
128 devices in a mesh: ob: 16 (over y_hi, z, core), pt: 8 (over x, y_lo).
Axes of the slice: x: 4, y: 4 (y_hi: 2, y_lo: 2; y = y_hi * 2 + y_lo), z: 4, core: 2. Of those that a mesh axis runs over, the one named last changes fastest.
Arguments:
- orbitals: float32 [512, 262144], P(('ob', 'pt')), may hold values from -32 to 32, as said below
- potential: float32 [262144], replicated, may hold values from 0 to 2
- cutoff: float32 [1], replicated, may hold values from 0.4 to 1
- eigvec: float32 [512, 512], replicated, may hold values from -3 to 3, as said below
Outputs:
- gram: float32 [512, 512], P(('ob', 'pt'))
- hamil_sub: float32 [512, 512], P(('ob', 'pt'))
- rotated: float32 [512, 262144], P(None, ('ob', 'pt'))
- residual: float32 [512, 262144], P(None, ('ob', 'pt'))
- ritz: float32 [512], replicated
Inputs may be any that keep to these rules, and one draw needn't show every extreme that they name: `orbitals`: each orbital is a rough field whose scale differs from orbital to orbital and from region to region of the grid. `eigvec`: A full-rank matrix with a unit-sized diagonal and independent off-diagonal entries.
All inputs are finite; a program needn't handle non-finite values.
Results may differ from a plain program's by a relative error of at most 0.00027.
Values sent between devices are 32-bit elements; how exact they have to be, the bound alone decides.
No kernel may reach another device: no remote copies, remote signals or barrier semaphores. Data moves between devices by JAX's collectives and lax.ppermute only.
A program may use at most 128 MiB of HBM per device.

v0:
```python
import jax
import jax.numpy as jnp
from jax import lax
from jax.sharding import PartitionSpec as P

G = 64
DEGREE = 12
NPTS = 262144


upper_bound = 8.0
quot_eps = 1e-06


def apply_ham(fields, potential):
    points = fields.shape[-1]
    plane_len = G * G
    x_pair = jnp.roll(fields, plane_len, axis=-1) + jnp.roll(fields, -plane_len, axis=-1)
    cube_view = fields.reshape(fields.shape[0], G, plane_len)
    y_pair = (jnp.roll(cube_view, G, axis=-1) + jnp.roll(cube_view, -G, axis=-1)).reshape(
        fields.shape
    )
    z_index = lax.broadcasted_iota(jnp.int32, (1, points), 1) % G
    z_lower = jnp.where(
        z_index == 0, jnp.roll(fields, 1 - G, axis=-1), jnp.roll(fields, 1, axis=-1)
    )
    z_upper = jnp.where(
        z_index == G - 1, jnp.roll(fields, G - 1, axis=-1), jnp.roll(fields, -1, axis=-1)
    )
    return -0.5 * (x_pair + y_pair + z_lower + z_upper - 6.0 * fields) + potential * fields


def chebyshev(fields, potential, cutoff):
    center = 0.5 * (upper_bound + cutoff[0])
    half_width = 0.5 * (upper_bound - cutoff[0])
    current = (apply_ham(fields, potential) - center * fields) / half_width

    def advance(turn_idx, carry):
        previous, present = carry
        following = 2.0 * (apply_ham(present, potential) - center * present) / half_width - previous
        return (present, following)

    previous, current = lax.fori_loop(0, DEGREE - 1, advance, (fields, current))
    return (current, apply_ham(current, potential))


def on_device(orbitals, potential, cutoff, eigvec):
    high = lax.Precision.HIGHEST
    filtered, applied = chebyshev(orbitals, potential, cutoff)
    total_orb = eigvec.shape[0]
    n_ob = lax.axis_size("ob")
    n_pt = lax.axis_size("pt")
    per_dev = total_orb // (n_ob * n_pt)
    rows_filt, rows_appl = (
        lax.all_to_all(filtered, ("ob", "pt"), split_axis=1, concat_axis=0, tiled=True),
        lax.all_to_all(applied, ("ob", "pt"), split_axis=1, concat_axis=0, tiled=True),
    )
    part_gram = jnp.dot(rows_filt, rows_filt.T, precision=high) / NPTS
    part_hamil = jnp.dot(rows_filt, rows_appl.T, precision=high) / NPTS
    gram, hamil_sub = (
        lax.psum_scatter(part_gram, ("ob", "pt"), scatter_dimension=0, tiled=True),
        lax.psum_scatter(part_hamil, ("ob", "pt"), scatter_dimension=0, tiled=True),
    )
    rotated = jnp.dot(eigvec.T, rows_filt, precision=high)
    rot_applied = jnp.dot(eigvec.T, rows_appl, precision=high)
    my_index = lax.axis_index(("ob", "pt"))
    my_rows = lax.dynamic_slice_in_dim(eigvec, my_index * per_dev, per_dev, 0)
    numer = jnp.sum(my_rows * jnp.dot(hamil_sub, eigvec, precision=high), axis=0)
    denom = jnp.sum(my_rows * jnp.dot(gram, eigvec, precision=high), axis=0)
    numer, denom = lax.psum((numer, denom), ("ob", "pt"))
    ritz = numer / (denom + quot_eps)
    residual = rot_applied - ritz[:, None] * rotated
    return (gram, hamil_sub, rotated, residual, ritz)


def solution(mesh):
    return jax.shard_map(
        on_device,
        mesh=mesh,
        in_specs=(P(("ob", "pt"), None), P(), P(), P()),
        out_specs=(
            P(("ob", "pt"), None),
            P(("ob", "pt"), None),
            P(None, ("ob", "pt")),
            P(None, ("ob", "pt")),
            P(),
        ),
        check_vma=False,
    )
```

profile of v0, /device:TPU:0, one launch (start us, length us, event | category | flops | bytes accessed | tf_op | source)
XLA Modules:
  0.0 1016.3 jit_solution(13360998057643080672)
XLA Ops:
  13.5 4.6 fusion.56
  28.6 4.7 copy.22
  33.3 24.7 %fusion.28 = f32[4,262144]{1,0:T(4,128)} fusion(f32[4,262144]{1,0:T(4,128)} %copy-done.2, f32[4,1]{1,0:T(4,128)S(1)} %get-tuple-element.162, f32[4,262143]{1,0:T(4,128)} %get-tuple-element.164, f32[4,262081]{1,0:T(4,128)} %get-tuple-element.158, f32[4,63]{1,0:T(4,128)S(1)} %get-tuple-element.160, f32[4,262143]{1,0:T(4,128)} %get-tuple-element.163, ...), kind=kLoop, calls=%fused_computation.47 | loop fusion | flops 20971520 | bytes 39321608 | tf_op jit(solution)/shard_map/div | solution.py:36
  58.0 528.4 %while.14 = (s32[]{:T(128)}, f32[4,262144]{1,0:T(4,128)}, f32[4,262144]{1,0:T(4,128)}, f32[262144]{0:T(1024)S(1)}, f32[]{:T(128)}, /*index=5*/f32[]{:T(128)}, s32[]{:T(128)}) while((s32[]{:T(128)}, f32[4,262144]{1,0:T(4,128)}, f32[4,262144]{1,0:T(4,128)}, f32[262144]{0:T(1024)S(1)}, f32[]{:T(128)}, /*index=5*/f32[]{:T(128)}, s32[]{:T(128)}) %tuple.84), condition=%wide.region_1.2_spmd, body=%wide.region_0.1_spmd.sunk | while | flops 28311552 | bytes 190840976 | solution.py:43
  58.3 4.6 copy.33
  81.5 20.9 %divide_subtract_fusion.2 = f32[4,262144]{1,0:T(4,128)S(1)} fusion(f32[4,262144]{1,0:T(4,128)S(1)} %copy-done.3, f32[4,262144]{1,0:T(4,128)S(1)} %copy-done, f32[4,1]{1,0:T(4,128)S(1)} %get-tuple-element.222, f32[4,262143]{1,0:T(4,128)} %get-tuple-element.223, f32[4,262081]{1,0:T(4,128)} %get-tuple-element.224, f32[4,63]{1,0:T(4,128)S(1)} %get-tuple-element.225, ...), kind=kLoop, calls=%fused_computation.clone.1 | loop fusion | flops 23068672 | bytes 43515912 | tf_op jit(solution)/shard_map/while/body/eval_jaxpr/sub | solution.py:40
  129.5 20.9 %divide_subtract_fusion.2 = f32[4,262144]{1,0:T(4,128)S(1)} fusion(f32[4,262144]{1,0:T(4,128)S(1)} %copy-done.3, f32[4,262144]{1,0:T(4,128)S(1)} %copy-done, f32[4,1]{1,0:T(4,128)S(1)} %get-tuple-element.222, f32[4,262143]{1,0:T(4,128)} %get-tuple-element.223, f32[4,262081]{1,0:T(4,128)} %get-tuple-element.224, f32[4,63]{1,0:T(4,128)S(1)} %get-tuple-element.225, ...), kind=kLoop, calls=%fused_computation.clone.1 | loop fusion | flops 23068672 | bytes 43515912 | tf_op jit(solution)/shard_map/while/body/eval_jaxpr/sub | solution.py:40
  177.5 20.9 %divide_subtract_fusion.2 = f32[4,262144]{1,0:T(4,128)S(1)} fusion(f32[4,262144]{1,0:T(4,128)S(1)} %copy-done.3, f32[4,262144]{1,0:T(4,128)S(1)} %copy-done, f32[4,1]{1,0:T(4,128)S(1)} %get-tuple-element.222, f32[4,262143]{1,0:T(4,128)} %get-tuple-element.223, f32[4,262081]{1,0:T(4,128)} %get-tuple-element.224, f32[4,63]{1,0:T(4,128)S(1)} %get-tuple-element.225, ...), kind=kLoop, calls=%fused_computation.clone.1 | loop fusion | flops 23068672 | bytes 43515912 | tf_op jit(solution)/shard_map/while/body/eval_jaxpr/sub | solution.py:40
  202.3 4.6 copy.33
  225.5 20.9 %divide_subtract_fusion.2 = f32[4,262144]{1,0:T(4,128)S(1)} fusion(f32[4,262144]{1,0:T(4,128)S(1)} %copy-done.3, f32[4,262144]{1,0:T(4,128)S(1)} %copy-done, f32[4,1]{1,0:T(4,128)S(1)} %get-tuple-element.222, f32[4,262143]{1,0:T(4,128)} %get-tuple-element.223, f32[4,262081]{1,0:T(4,128)} %get-tuple-element.224, f32[4,63]{1,0:T(4,128)S(1)} %get-tuple-element.225, ...), kind=kLoop, calls=%fused_computation.clone.1 | loop fusion | flops 23068672 | bytes 43515912 | tf_op jit(solution)/shard_map/while/body/eval_jaxpr/sub | solution.py:40
  273.5 20.9 %divide_subtract_fusion.2 = f32[4,262144]{1,0:T(4,128)S(1)} fusion(f32[4,262144]{1,0:T(4,128)S(1)} %copy-done.3, f32[4,262144]{1,0:T(4,128)S(1)} %copy-done, f32[4,1]{1,0:T(4,128)S(1)} %get-tuple-element.222, f32[4,262143]{1,0:T(4,128)} %get-tuple-element.223, f32[4,262081]{1,0:T(4,128)} %get-tuple-element.224, f32[4,63]{1,0:T(4,128)S(1)} %get-tuple-element.225, ...), kind=kLoop, calls=%fused_computation.clone.1 | loop fusion | flops 23068672 | bytes 43515912 | tf_op jit(solution)/shard_map/while/body/eval_jaxpr/sub | solution.py:40
  321.4 20.9 %divide_subtract_fusion.2 = f32[4,262144]{1,0:T(4,128)S(1)} fusion(f32[4,262144]{1,0:T(4,128)S(1)} %copy-done.3, f32[4,262144]{1,0:T(4,128)S(1)} %copy-done, f32[4,1]{1,0:T(4,128)S(1)} %get-tuple-element.222, f32[4,262143]{1,0:T(4,128)} %get-tuple-element.223, f32[4,262081]{1,0:T(4,128)} %get-tuple-element.224, f32[4,63]{1,0:T(4,128)S(1)} %get-tuple-element.225, ...), kind=kLoop, calls=%fused_computation.clone.1 | loop fusion | flops 23068672 | bytes 43515912 | tf_op jit(solution)/shard_map/while/body/eval_jaxpr/sub | solution.py:40
  369.4 20.9 %divide_subtract_fusion.2 = f32[4,262144]{1,0:T(4,128)S(1)} fusion(f32[4,262144]{1,0:T(4,128)S(1)} %copy-done.3, f32[4,262144]{1,0:T(4,128)S(1)} %copy-done, f32[4,1]{1,0:T(4,128)S(1)} %get-tuple-element.222, f32[4,262143]{1,0:T(4,128)} %get-tuple-element.223, f32[4,262081]{1,0:T(4,128)} %get-tuple-element.224, f32[4,63]{1,0:T(4,128)S(1)} %get-tuple-element.225, ...), kind=kLoop, calls=%fused_computation.clone.1 | loop fusion | flops 23068672 | bytes 43515912 | tf_op jit(solution)/shard_map/while/body/eval_jaxpr/sub | solution.py:40
  417.4 20.9 %divide_subtract_fusion.2 = f32[4,262144]{1,0:T(4,128)S(1)} fusion(f32[4,262144]{1,0:T(4,128)S(1)} %copy-done.3, f32[4,262144]{1,0:T(4,128)S(1)} %copy-done, f32[4,1]{1,0:T(4,128)S(1)} %get-tuple-element.222, f32[4,262143]{1,0:T(4,128)} %get-tuple-element.223, f32[4,262081]{1,0:T(4,128)} %get-tuple-element.224, f32[4,63]{1,0:T(4,128)S(1)} %get-tuple-element.225, ...), kind=kLoop, calls=%fused_computation.clone.1 | loop fusion | flops 23068672 | bytes 43515912 | tf_op jit(solution)/shard_map/while/body/eval_jaxpr/sub | solution.py:40
  465.4 20.9 %divide_subtract_fusion.2 = f32[4,262144]{1,0:T(4,128)S(1)} fusion(f32[4,262144]{1,0:T(4,128)S(1)} %copy-done.3, f32[4,262144]{1,0:T(4,128)S(1)} %copy-done, f32[4,1]{1,0:T(4,128)S(1)} %get-tuple-element.222, f32[4,262143]{1,0:T(4,128)} %get-tuple-element.223, f32[4,262081]{1,0:T(4,128)} %get-tuple-element.224, f32[4,63]{1,0:T(4,128)S(1)} %get-tuple-element.225, ...), kind=kLoop, calls=%fused_computation.clone.1 | loop fusion | flops 23068672 | bytes 43515912 | tf_op jit(solution)/shard_map/while/body/eval_jaxpr/sub | solution.py:40
  513.4 20.9 %divide_subtract_fusion.2 = f32[4,262144]{1,0:T(4,128)S(1)} fusion(f32[4,262144]{1,0:T(4,128)S(1)} %copy-done.3, f32[4,262144]{1,0:T(4,128)S(1)} %copy-done, f32[4,1]{1,0:T(4,128)S(1)} %get-tuple-element.222, f32[4,262143]{1,0:T(4,128)} %get-tuple-element.223, f32[4,262081]{1,0:T(4,128)} %get-tuple-element.224, f32[4,63]{1,0:T(4,128)S(1)} %get-tuple-element.225, ...), kind=kLoop, calls=%fused_computation.clone.1 | loop fusion | flops 23068672 | bytes 43515912 | tf_op jit(solution)/shard_map/while/body/eval_jaxpr/sub | solution.py:40
  561.4 20.9 %divide_subtract_fusion.2 = f32[4,262144]{1,0:T(4,128)S(1)} fusion(f32[4,262144]{1,0:T(4,128)S(1)} %copy-done.3, f32[4,262144]{1,0:T(4,128)S(1)} %copy-done, f32[4,1]{1,0:T(4,128)S(1)} %get-tuple-element.222, f32[4,262143]{1,0:T(4,128)} %get-tuple-element.223, f32[4,262081]{1,0:T(4,128)} %get-tuple-element.224, f32[4,63]{1,0:T(4,128)S(1)} %get-tuple-element.225, ...), kind=kLoop, calls=%fused_computation.clone.1 | loop fusion | flops 23068672 | bytes 43515912 | tf_op jit(solution)/shard_map/while/body/eval_jaxpr/sub | solution.py:40
  586.3 4.6 copy.29
  609.9 23.3 %fusion.26 = f32[4,262144]{1,0:T(4,128)S(1)} fusion(f32[4,262144]{1,0:T(4,128)S(1)} %bitcast.64, f32[4,258048]{1,0:T(4,128)} %get-tuple-element.142, f32[4,4096]{1,0:T(4,128)S(1)} %get-tuple-element.144, f32[4,4096]{1,0:T(4,128)S(1)} %get-tuple-element.143, f32[4,258048]{1,0:T(4,128)} %get-tuple-element.141, f32[4,63]{1,0:T(4,128)S(1)} %get-tuple-element.138, ...), kind=kLoop, calls=%fused_computation.41 | loop fusion | flops 17825792 | bytes 39321600 | tf_op jit(solution)/shard_map/add | solution.py:30
  633.2 63.7 %all_to_all.38 = f32[4,128,2048]{2,0,1:T(4,128)} all-to-all(f32[4,128,2048]{2,0,1:T(4,128)S(1)} %bitcast.65), channel_id=1, replica_groups=mesh['ob'=16,'pt'=8] {'ob','pt'}, dimensions={1} | all-to-all | bytes 8388608 | tf_op jit(solution)/shard_map/all_to_all | solution.py:56
  696.8 6.2 all-to-all-start
  703.1 5.7 all_to_all.35
  708.8 46.4 %all-to-all-done = f32[4,128,2048]{2,0,1:T(4,128)} async-done(((f32[4,128,2048]{2,0,1:T(4,128)}), f32[4,128,2048]{2,0,1:T(4,128)}, u32[]{:S(2)}, u32[]{:S(2)}) %all-to-all-start) | async-done | bytes 4194336 | tf_op jit(solution)/shard_map/all_to_all | solution.py:55
  755.2 5.3 all_to_all.31
  760.5 10.5 %convolution_multiply_fusion.1 = f32[512,512]{1,0:T(8,128)} fusion(f32[512,2048]{1,0:T(8,128)} %all_to_all.31), kind=kOutput, calls=%fused_computation.51 | convolution fusion | flops 6442713088 | bytes 5242880 | tf_op jit(solution)/shard_map/dot_general | solution.py:58
  771.0 7.9 convolution_multiply_fusion
  779.0 10.1 convolution_bitcast_fusion
  789.1 5.4 copy.17
  794.5 132.4 %all-reduce.6.cloned.1.call-done = (f32[512,512]{1,0:T(8,128)}, f32[512,512]{1,0:T(8,128)}) async-done(((f32[512,512]{1,0:T(8,128)}, f32[512,512]{1,0:T(8,128)}), (f32[512,512]{1,0:T(8,128)}, f32[512,512]{1,0:T(8,128)})) %all-reduce.6.cloned.1.call-update) | async-done | bytes 2097168
  929.6 63.8 %all-reduce.2 = (f32[512]{0:T(512)S(1)}, f32[512]{0:T(512)S(1)}) all-reduce(f32[512]{0:T(512)S(1)} %fusion.29, f32[512]{0:T(512)S(1)} %fusion.30), channel_id=1, replica_groups=mesh['ob'=16,'pt'=8] {'ob','pt'}, use_global_device_ids=true, to_apply=%region_5.6 | all-reduce | flops 1024 | bytes 8192 | tf_op jit(solution)/shard_map/psum | solution.py:70
  993.4 10.6 %bitcast_subtract_fusion = f32[512,2048]{0,1:T(8,128)} fusion(f32[512,2048]{0,1:T(8,128)} %convolution_bitcast_fusion, f32[512,2048]{1,0:T(8,128)} %all_to_all.35, f32[512,512]{1,0:T(8,128)S(1)} %copy-done.7, f32[512]{0:T(512)S(1)} %add_divide_fusion), kind=kOutput, calls=%fused_computation.46 | convolution fusion | flops 6444548096 | bytes 13633536 | tf_op jit(solution)/shard_map/dot_general | solution.py:65
  1004.0 5.3 copy.18
  (252 shorter events, 326.0 us)
Async XLA Ops:
  9.4 16.8 %copy-start.2 = (f32[4,262144]{1,0:T(4,128)}, f32[4,262144]{1,0:T(4,128)S(1)}, u32[]{:S(2)}) copy-start(f32[4,262144]{1,0:T(4,128)S(1)} %copy.48) | copy-start | bytes 12582916
  26.6 6.7 copy-start.9
  26.6 6.7 copy-start.11
  28.6 4.7 copy-start.5
  65.9 2.7 copy-start
  76.9 4.6 copy-start.3
  113.9 2.7 copy-start
  124.8 4.6 copy-start.3
  161.9 2.7 copy-start
  172.8 4.6 copy-start.3
  209.9 2.7 copy-start
  220.8 4.6 copy-start.3
  268.8 4.6 copy-start.3
  316.8 4.6 copy-start.3
  353.9 2.7 copy-start
  364.8 4.6 copy-start.3
  401.8 2.7 copy-start
  412.8 4.6 copy-start.3
  460.7 4.6 copy-start.3
  508.7 4.6 copy-start.3
  556.7 4.6 copy-start.3
  607.1 2.7 copy-start.8
  607.1 2.7 copy-start.10
  607.1 2.7 copy-start.12
  696.8 58.4 %all-to-all-start = ((f32[4,128,2048]{2,0,1:T(4,128)}), f32[4,128,2048]{2,0,1:T(4,128)}, u32[]{:S(2)}, u32[]{:S(2)}) async-start(f32[4,128,2048]{2,0,1:T(4,128)} %bitcast.53), calls=%async_computation | async-start | bytes 8388608 | tf_op jit(solution)/shard_map/all_to_all | solution.py:55
  703.1 223.8 %all-reduce.6.cloned.1.call-start = ((), (), s32[]{:S(2)}) async-start(), calls=%async_computation.2 | async-start | bytes 4194304
  760.5 10.5 %copy-start.4 = (f32[512,2048]{1,0:T(8,128)S(1)}, f32[512,2048]{1,0:T(8,128)}, u32[]{:S(2)}) copy-start(f32[512,2048]{1,0:T(8,128)} %all_to_all.31) | copy-start | bytes 12582916
  760.5 10.5 %copy-start.6 = (f32[512,2048]{1,0:T(8,128)S(1)}, f32[512,2048]{1,0:T(8,128)}, u32[]{:S(2)}) copy-start(f32[512,2048]{1,0:T(8,128)} %all_to_all.35) | copy-start | bytes 12582916
  771.0 8.0 copy-start.7
  927.6 76.4 %copy-start.13 = (f32[4,512]{1,0:T(4,128)}, f32[4,512]{1,0:T(4,128)S(1)}, u32[]{:S(2)}) copy-start(f32[4,512]{1,0:T(4,128)S(1)} %constant_dynamic-slice_fusion) | copy-start | bytes 24580
  928.3 75.6 %copy-start.14 = (f32[4,512]{1,0:T(4,128)}, f32[4,512]{1,0:T(4,128)S(1)}, u32[]{:S(2)}) copy-start(f32[4,512]{1,0:T(4,128)S(1)} %constant_dynamic-slice_fusion.1) | copy-start | bytes 24580
  993.4 10.6 %copy-start.15 = (f32[512]{0:T(512)}, f32[512]{0:T(512)S(1)}, u32[]{:S(2)}) copy-start(f32[512]{0:T(512)S(1)} %add_divide_fusion) | copy-start | bytes 6148
  (6 other events, 15.8 us)
Sparse Core Ops, SparseCore 0:
  779.1 147.7 all-reduce.5
where the time goes:
time: 1020 us
  local copies, waits for them, and re-layouts  348 us (34%)
  other arithmetic  299 us (29%)
  waiting for transfers between devices  179 us (18%)
  blocking collectives  127 us (12%)
  matrix products  40.3 us (4%)
  between operations  15.1 us (1%)
    sub x11, other arithmetic, advance(): 2.0 * (apply_ham(present, potential) - center * present) / half_width  229 us
    unnamed x2, waiting for transfers between devices  132 us
    while x88, local copies, waits for them, and re-layouts  124 us
    psum x1, blocking collectives, on_device(): numer, denom = lax.psum((numer, denom), ('ob', 'pt'))  63.8 us
    all_to_all x1, blocking collectives, on_device(): lax.all_to_all(applied, ('ob', 'pt'), split_axis=1, concat_axis=0, tiled=...  63.7 us
    slice x24, local copies, waits for them, and re-layouts, apply_ham(): jnp.roll(fields, 1 - G, axis=-1)  54.5 us
    slice x24, local copies, waits for them, and re-layouts, apply_ham(): jnp.roll(fields, plane_len, axis=-1) + jnp.roll(fields, -plane_len, axis=-1)  49.1 us
    all_to_all x1, waiting for transfers between devices, on_device(): lax.all_to_all(filtered, ('ob', 'pt'), split_axis=1, concat_axis=0, tiled...  46.4 us
  transfers between devices with their start and end apart: 2, of which 2 were waited for; matrix products, arithmetic and copies ran while one was open for 2% of the time, Pallas kernels for 0%

commit v1 on v0

v1 whole, which is shorter than its diff:
```python
import functools

import jax
import jax.numpy as jnp
from jax import lax
from jax.experimental import pallas as pl
from jax.experimental.pallas import tpu as pltpu
from jax.sharding import PartitionSpec as P

NPTS = 262144
CHUNKS = (2, 2)
AXES = ("ob", "pt")
upper_bound = 8.0
quot_eps = 1e-06

YB = 16

def lane_roll(v, s):
    n = v.shape[0]
    return pltpu.roll(v.reshape(n * 8, 128), s % 128, 1).reshape(n, 8, 128)

def sub_roll(v, s):
    return pltpu.roll(v, s % 8, 1)

def filter_kernel(first, count, x_ref, pot_ref, cut_ref, out_ref, abuf, bbuf, wbuf):
    cut = cut_ref[0]
    center = 0.5 * (upper_bound + cut)
    half_width = 0.5 * (upper_bound - cut)
    alpha = -1.0 / half_width
    lane = lax.broadcasted_iota(jnp.int32, (YB, 8, 128), 2)
    low_half = lax.broadcasted_iota(jnp.int32, (8, 128), 1) < 64
    z_first = (lane & 63) == 0
    z_last = (lane & 63) == 63

    def to_blocks(load, store):
        def body(xl, _):
            for yp in range(16):
                a = load(xl * 32 + yp)
                b = load(xl * 32 + 16 + yp)
                ra, rb = pltpu.roll(a, 64, 1), pltpu.roll(b, 64, 1)
                store(xl, 2 * yp, jnp.where(low_half, a, rb))
                store(xl, 2 * yp + 1, jnp.where(low_half, ra, b))
            return 0
        lax.fori_loop(0, 8, body, 0)

    def w_store(xl, y, v):
        wbuf[xl, y] = v * (2.0 / half_width)
    to_blocks(lambda r: pot_ref[pl.ds(r, 8, stride=256), :] + (3.0 - center), w_store)


    def halo(buf):
        for xl in range(8):
            buf[xl, 0] = pltpu.roll(buf[xl, 32], 64, 1)
            buf[xl, 33] = pltpu.roll(buf[xl, 1], 64, 1)

    def sweep(cur, emit):
        def block(yb, _):
            y0 = yb * YB
            def at(xl):
                return cur[xl, pl.ds(y0 + 1, YB)]
            below = sub_roll(at(7), 1)
            here = at(0)
            wrap = sub_roll(here, -1)
            for xl in range(8):
                above = at(xl + 1) if xl < 7 else wrap
                lo = cur[xl, pl.ds(y0, 1)]
                hi = cur[xl, pl.ds(y0 + YB + 1, 1)]
                ym = jnp.concatenate([lo, here[:YB - 1]], 0)
                yp = jnp.concatenate([here[1:], hi], 0)
                zm = jnp.where(z_first, lane_roll(here, -63), lane_roll(here, 1))
                zp = jnp.where(z_last, lane_roll(here, 63), lane_roll(here, -1))
                s = ((below + above) + (ym + yp)) + (zm + zp)
                t = alpha * s + wbuf[xl, pl.ds(y0, YB)] * here
                emit(xl, y0, here, t)
                below, here = here, above
            return 0
        lax.fori_loop(0, 32 // YB, block, 0)

    def advance(cur, old):
        def emit(xl, y0, v, t):
            old[xl, pl.ds(y0 + 1, YB)] = t - old[xl, pl.ds(y0 + 1, YB)]
        sweep(cur, emit)
        halo(old)

    def one(o, _):
        orb = first + o
        def y_store(xl, y, v):
            abuf[xl, y + 1] = v
        to_blocks(lambda r: x_ref[pl.ds(r * 4 + orb, 8, stride=1024), :], y_store)
        halo(abuf)

        def emit_first(xl, y0, v, t):
            bbuf[xl, pl.ds(y0 + 1, YB)] = 0.5 * t
        sweep(abuf, emit_first)
        halo(bbuf)

        def pair(k, _):
            advance(bbuf, abuf)
            @pl.when(k < 5)
            def _():
                advance(abuf, bbuf)
            return 0
        lax.fori_loop(0, 6, pair, 0)

        def emit_last(xl, y0, v, t):
            ap = (0.5 * half_width) * t + center * v
            yp0 = y0 // 2
            for which, val in ((0, v), (1, ap)):
                for j in range(YB // 2):
                    e, d = val[2 * j], val[2 * j + 1]
                    re, rd = pltpu.roll(e, 64, 1), pltpu.roll(d, 64, 1)
                    a = jnp.where(low_half, e, rd)
                    b = jnp.where(low_half, re, d)
                    q = (2 * o + which) * 16 + yp0 + j
                    out_ref[pl.ds(2 * xl * (32 * count) + q, 8, stride=512 * count), :] = a
                    out_ref[pl.ds((2 * xl + 1) * (32 * count) + q, 8, stride=512 * count), :] = b
        sweep(abuf, emit_last)
        return 0
    lax.fori_loop(0, count, one, 0)


def run_filter(orb, pot, cut, first, count):
    return pl.pallas_call(
        functools.partial(filter_kernel, first, count),
        out_shape=jax.ShapeDtypeStruct((128 * 2 * count * 16, 128), jnp.float32),
        in_specs=[
            pl.BlockSpec(memory_space=pltpu.VMEM),
            pl.BlockSpec(memory_space=pltpu.VMEM),
            pl.BlockSpec(memory_space=pltpu.SMEM),
        ],
        out_specs=pl.BlockSpec(memory_space=pltpu.VMEM),
        scratch_shapes=[
            pltpu.VMEM((8, 34, 8, 128), jnp.float32),
            pltpu.VMEM((8, 34, 8, 128), jnp.float32),
            pltpu.VMEM((8, 32, 8, 128), jnp.float32),
        ],
        compiler_params=pltpu.CompilerParams(vmem_limit_bytes=30 << 20),
        cost_estimate=pl.CostEstimate(
            flops=count * 13 * NPTS * 40, bytes_accessed=count << 21, transcendentals=0
        ),
        name="filter",
    )(orb, pot, cut)


def project_kernel(*refs):
    n = len(CHUNKS)
    chunks, (e_ref, rot_ref, rota_ref, pay_ref, e3, gram, hamil, acc_n, acc_d) = refs[:n], refs[n:]
    where = [(c, o) for c in range(n) for o in range(CHUNKS[c])]
    e = e_ref[...]
    e_hi = e.astype(jnp.bfloat16)
    e3[:, :512] = e_hi
    e3[:, 512:1024] = e_hi
    e3[:, 1024:] = (e - e_hi.astype(jnp.float32)).astype(jnp.bfloat16)
    gram[...] = jnp.zeros_like(gram)
    hamil[...] = jnp.zeros_like(hamil)
    acc_n[...] = jnp.zeros_like(acc_n)
    acc_d[...] = jnp.zeros_like(acc_d)

    def fetch(t, which):
        cols = []
        for h in range(2):
            rows = []
            for c, o in where:
                rows.append(
                    chunks[c][pl.ds((2 * o + which) * 16 + 2 * t + h, 128, stride=32 * CHUNKS[c]), :]
                )
            cols.append(jnp.concatenate(rows, 0))
        x = jnp.concatenate(cols, 1)
        hi = x.astype(jnp.bfloat16)
        lo = (x - hi.astype(jnp.float32)).astype(jnp.bfloat16)
        return hi, lo

    def nt(a, b):
        return lax.dot_general(a, b, (((1,), (1,)), ((), ())), preferred_element_type=jnp.float32)

    def body(t, _):
        fh, fl = fetch(t, 0)
        ah, al = fetch(t, 1)
        left = jnp.concatenate([fh, fh, fl], 1)
        gram[...] += nt(left, jnp.concatenate([fh, fl, fh], 1))
        hamil[...] += nt(left, jnp.concatenate([ah, al, ah], 1))
        rot = jnp.dot(e3[...], jnp.concatenate([fh, fl, fh], 0), preferred_element_type=jnp.float32)
        rota = jnp.dot(e3[...], jnp.concatenate([ah, al, ah], 0), preferred_element_type=jnp.float32)
        cols = pl.ds(pl.multiple_of(t * 256, 256), 256)
        rot_ref[:, cols] = rot
        rota_ref[:, cols] = rota
        pn, pd = rot * rota, rot * rot
        acc_n[...] += pn[:, :128] + pn[:, 128:]
        acc_d[...] += pd[:, :128] + pd[:, 128:]
        return 0

    lax.fori_loop(0, 8, body, 0)
    scale = 1.0 / NPTS
    for m, mat in enumerate((gram, hamil)):
        for o in range(4):
            for q in range(4):
                pay_ref[pl.ds(m * 16 + o * 4 + q, 128, stride=40), :] = (
                    mat[128 * o : 128 * o + 128, 128 * q : 128 * q + 128] * scale
                )
    for m, acc in enumerate((acc_n, acc_d)):
        for q in range(4):
            row = jnp.sum(acc[128 * q : 128 * q + 128, :].T, axis=0, keepdims=True) * scale
            pay_ref[pl.ds(32 + m * 4 + q, 128, stride=40), :] = jnp.broadcast_to(row, (128, 128))


def run_project(chunks, et):
    vm = pl.BlockSpec(memory_space=pltpu.VMEM)
    return pl.pallas_call(
        project_kernel,
        out_shape=(
            jax.ShapeDtypeStruct((512, 2048), jnp.float32),
            jax.ShapeDtypeStruct((512, 2048), jnp.float32),
            jax.ShapeDtypeStruct((128 * 40, 128), jnp.float32),
        ),
        in_specs=[vm] * (len(chunks) + 1),
        out_specs=(vm, vm, vm),
        scratch_shapes=[
            pltpu.VMEM((512, 1536), jnp.bfloat16),
            pltpu.VMEM((512, 512), jnp.float32),
            pltpu.VMEM((512, 512), jnp.float32),
            pltpu.VMEM((512, 128), jnp.float32),
            pltpu.VMEM((512, 128), jnp.float32),
        ],
        compiler_params=pltpu.CompilerParams(vmem_limit_bytes=50 << 20),
        cost_estimate=pl.CostEstimate(flops=13 << 30, bytes_accessed=20 << 20, transcendentals=0),
        name="project",
    )(*chunks, et)


def on_device(orbitals, potential, cutoff, eigvec):
    orb = orbitals.reshape(4, 2048, 128).transpose(1, 0, 2).reshape(8192, 128)
    pot = potential.reshape(2048, 128)
    et = eigvec.reshape(128, 4, 512).transpose(2, 1, 0).reshape(512, 512)
    received = []
    first = 0
    for count in CHUNKS:
        sent = run_filter(orb, pot, cutoff, first, count).reshape(128, 32 * count, 128)
        got = lax.all_to_all(sent, AXES, split_axis=0, concat_axis=0, tiled=True)
        received.append(got.reshape(128 * 32 * count, 128))
        first += count
    rotated, rot_applied, pay = run_project(received, et)
    pay = lax.all_to_all(pay.reshape(128, 40, 128), AXES, split_axis=0, concat_axis=0, tiled=True)
    total = jnp.sum(pay, axis=0)
    mats = total[:32].reshape(2, 4, 4, 128).transpose(0, 1, 3, 2).reshape(2, 4, 512)
    numer = total[32:36].reshape(512)
    denom = total[36:40].reshape(512)
    ritz = numer / (denom + quot_eps)
    residual = rot_applied - ritz[:, None] * rotated
    return (mats[0], mats[1], rotated, residual, ritz)


def solution(mesh):
    return jax.shard_map(
        on_device,
        mesh=mesh,
        in_specs=(P(AXES, None), P(), P(), P()),
        out_specs=(P(AXES, None), P(AXES, None), P(None, AXES), P(None, AXES), P()),
        check_vma=False,
    )
```

time: 1020 us -> 247 us (0.24)
  local copies, waits for them, and re-layouts: 348 us -> 12.4 us
  other arithmetic: 299 us -> 6.17 us
  waiting for transfers between devices: 179 us -> 57.4 us
  Pallas kernels: 0 us -> 110 us
  blocking collectives: 127 us -> 41.2 us
  matrix products: 40.3 us -> 0 us
  between operations: 15.1 us -> 1.43 us
  starting transfers between devices: 6.25 us -> 17.9 us
    sub x11 -> x1, other arithmetic: 229 us -> 5.95 us  [on_device(): residual = rot_applied - ritz[:, None] * rotated]
    slice x104 -> x4, local copies, waits for them, and re-layouts: 184 us -> 0.29 us  [the longest x3 0.29 us: on_device(): return (mats[0], mats[1], rotated, residual, ritz)]
    unnamed x2 -> x0, waiting for transfers between devices: 132 us -> none
    while x88 -> x0, local copies, waits for them, and re-layouts: 124 us -> none
    pallas_call x0 -> x3, Pallas kernels: none -> 110 us  [the longest x2 83.6 us: run_filter(): pl.pallas_call(functools.partial(filter_kernel, first, count), out_shape=...]
    psum x1 -> x0, blocking collectives: 63.8 us -> none  [on_device(): numer, denom = lax.psum((numer, denom), ('ob', 'pt'))]
    dot_general x6 -> x0, matrix products: 40.3 us -> none  [the longest x1 10.6 us: on_device(): rot_applied = jnp.dot(eigvec.T, rows_appl, precision=high)]
    div x1 -> x0, other arithmetic: 24.7 us -> none  [chebyshev(): current = (apply_ham(fields, potential) - center * fields) / half_width]
  transfers between devices with their start and end apart: 2 -> 2, of which waited for: 2 -> 2; matrix products, arithmetic and copies ran while one was open for 2% -> 0% of each run, Pallas kernels for 0% -> 17%
where the time goes in v1:
time: 247 us; the launch traced here: 246 us
  Pallas kernels  110 us (45%)
  waiting for transfers between devices  57.4 us (23%)
  blocking collectives  41.2 us (17%)
  starting transfers between devices  17.9 us (7%)
  local copies, waits for them, and re-layouts  12.4 us (5%)
  other arithmetic  6.17 us (2%)
    pallas_call x2, Pallas kernels, run_filter(): pl.pallas_call(functools.partial(filter_kernel, first, count), out_shape=...  83.6 us
    all_to_all x2, waiting for transfers between devices, on_device(): got = lax.all_to_all(sent, AXES, split_axis=0, concat_axis=0, tiled=True)  57.4 us
    all_to_all x1, blocking collectives, on_device(): lax.all_to_all(pay.reshape(128, 40, 128), AXES, split_axis=0, concat_axis...  41.2 us
    pallas_call x1, Pallas kernels, run_project(): pl.pallas_call(project_kernel, out_shape=(jax.ShapeDtypeStruct((512, 2048...  26.2 us
    all_to_all x2, starting transfers between devices, on_device(): got = lax.all_to_all(sent, AXES, split_axis=0, concat_axis=0, tiled=True)  17.9 us
    unnamed x17, local copies, waits for them, and re-layouts  9.69 us
    sub x1, other arithmetic, on_device(): residual = rot_applied - ritz[:, None] * rotated  5.95 us
  transfers between devices with their start and end apart: 2, of which 2 were waited for; matrix products, arithmetic and copies ran while one was open for 0% of the time, Pallas kernels for 17%

profile of v1, /device:TPU:0, one launch (start us, length us, event | category | flops | bytes accessed | tf_op | source)
XLA Modules:
  0.0 246.2 jit_solution(18420234934428445671)
XLA Ops:
  1.3 0.0 copy-start
  1.3 2.2 copy-done
  3.5 0.0 copy-start.4
  3.5 1.2 copy-done.4
  4.7 41.8 %filter.3 = f32[8192,128]{1,0:T(8,128)S(1)} custom-call(f32[8192,128]{1,0:T(8,128)S(1)} %bitcast.25, f32[2048,128]{1,0:T(8,128)S(1)} %bitcast.29, f32[1]{0:T(128)S(6)} %copy.18.cut_ref), custom_call_target="tpu_custom_call" | custom-call | flops 272629760 | bytes 4194304 | tf_op jit(solution)/shard_map/filter/pallas_call | solution.py:123
  46.5 0.0 copy-start.3
  46.5 2.0 copy-done.3
  48.5 0.0 copy-start.5
  48.5 11.7 %all-to-all-start.1 = ((f32[128,64,128]{2,1,0:T(8,128)}), f32[128,64,128]{2,1,0:T(8,128)}, u32[]{:S(2)}, u32[]{:S(2)}) async-start(f32[128,64,128]{2,1,0:T(8,128)} %bitcast.28), calls=%async_computation.1 | async-start | bytes 8388608 | tf_op jit(solution)/shard_map/all_to_all | solution.py:238
  60.2 0.0 copy-done.5
  60.2 0.0 copy-start.1
  60.2 2.2 copy-done.1
  62.4 41.8 %filter.2 = f32[8192,128]{1,0:T(8,128)S(1)} custom-call(f32[8192,128]{1,0:T(8,128)S(1)} %bitcast.26, f32[2048,128]{1,0:T(8,128)S(1)} %bitcast.30, f32[1]{0:T(128)S(6)} %copy.18.cut_ref), custom_call_target="tpu_custom_call" | custom-call | flops 272629760 | bytes 4194304 | tf_op jit(solution)/shard_map/filter/pallas_call | solution.py:123
  104.2 0.0 copy-start.2
  104.2 2.0 copy-done.2
  106.2 6.2 %all-to-all-done.1 = f32[128,64,128]{2,1,0:T(8,128)} async-done(((f32[128,64,128]{2,1,0:T(8,128)}), f32[128,64,128]{2,1,0:T(8,128)}, u32[]{:S(2)}, u32[]{:S(2)}) %all-to-all-start.1) | async-done | bytes 4194336 | tf_op jit(solution)/shard_map/all_to_all | solution.py:238
  112.4 0.0 copy-start.6
  112.4 6.2 %all-to-all-start = ((f32[128,64,128]{2,1,0:T(8,128)}), f32[128,64,128]{2,1,0:T(8,128)}, u32[]{:S(2)}, u32[]{:S(2)}) async-start(f32[128,64,128]{2,1,0:T(8,128)} %bitcast.27), calls=%async_computation | async-start | bytes 8388608 | tf_op jit(solution)/shard_map/all_to_all | solution.py:238
  118.6 0.0 copy-done.6
  118.6 0.3 reshape.70
  118.9 0.6 copy.12
  119.5 0.1 copy.17
  119.6 51.2 %all-to-all-done = f32[128,64,128]{2,1,0:T(8,128)} async-done(((f32[128,64,128]{2,1,0:T(8,128)}), f32[128,64,128]{2,1,0:T(8,128)}, u32[]{:S(2)}, u32[]{:S(2)}) %all-to-all-start) | async-done | bytes 4194336 | tf_op jit(solution)/shard_map/all_to_all | solution.py:238
  170.8 26.2 %project.1 = (f32[512,2048]{1,0:T(8,128)}, f32[512,2048]{1,0:T(8,128)}, f32[5120,128]{1,0:T(8,128)S(1)}) custom-call(f32[8192,128]{1,0:T(8,128)} %bitcast.5.refs_0_, f32[8192,128]{1,0:T(8,128)} %bitcast.9.refs_1_, f32[512,512]{1,0:T(8,128)S(1)} %bitcast.32), custom_call_target="tpu_custom_call" | custom-call | flops 13958643712 | bytes 20971520 | tf_op jit(solution)/shard_map/project/pallas_call | solution.py:208
  196.9 41.2 %all_to_all.15 = f32[128,40,128]{2,1,0:T(8,128)S(1)} all-to-all(f32[128,40,128]{2,1,0:T(8,128)S(1)} %bitcast.31), channel_id=1, replica_groups=mesh['ob'=16,'pt'=8] {'ob','pt'}, dimensions={0} | all-to-all | bytes 5242880 | tf_op jit(solution)/shard_map/all_to_all | solution.py:242
  238.2 0.2 reduce_sum.9
  238.4 0.1 copy.14
  238.6 0.8 squeeze.7
  239.4 0.1 copy.13
  239.5 0.8 squeeze.6
  240.3 5.9 %multiply_subtract_fusion = f32[512,2048]{1,0:T(8,128)} fusion(f32[512,2048]{1,0:T(8,128)} %get-tuple-element.10, f32[512,2048]{1,0:T(8,128)} %get-tuple-element.5, f32[512]{0:T(512)S(1)} %fusion.1), kind=kLoop, calls=%fused_computation | loop fusion | flops 2097152 | bytes 12584960 | tf_op jit(solution)/shard_map/sub | solution.py:248
  246.2 0.0 copy-done.7
  (4 shorter events, 0.0 us)
Async XLA Ops:
  1.3 2.2 copy-start
  3.5 1.2 copy-start.4
  46.5 2.0 copy-start.3
  48.5 11.7 %copy-start.5 = (f32[262144]{0:T(1024)S(1)}, f32[262144]{0:T(1024)}, u32[]{:S(2)}) copy-start(f32[262144]{0:T(1024)} %param.5) | copy-start | bytes 3145732
  48.5 63.9 %all-to-all-start.1 = ((f32[128,64,128]{2,1,0:T(8,128)}), f32[128,64,128]{2,1,0:T(8,128)}, u32[]{:S(2)}, u32[]{:S(2)}) async-start(f32[128,64,128]{2,1,0:T(8,128)} %bitcast.28), calls=%async_computation.1 | async-start | bytes 8388608 | tf_op jit(solution)/shard_map/all_to_all | solution.py:238
  60.2 2.2 copy-start.1
  104.2 2.0 copy-start.2
  112.4 6.2 %copy-start.6 = (f32[512,512]{1,0:T(8,128)S(1)}, f32[512,512]{1,0:T(8,128)}, u32[]{:S(2)}) copy-start(f32[512,512]{1,0:T(8,128)} %param.7) | copy-start | bytes 3145732
  112.4 58.4 %all-to-all-start = ((f32[128,64,128]{2,1,0:T(8,128)}), f32[128,64,128]{2,1,0:T(8,128)}, u32[]{:S(2)}, u32[]{:S(2)}) async-start(f32[128,64,128]{2,1,0:T(8,128)} %bitcast.27), calls=%async_computation | async-start | bytes 8388608 | tf_op jit(solution)/shard_map/all_to_all | solution.py:238
  238.4 7.8 %copy-start.7 = (f32[512]{0:T(512)}, f32[512]{0:T(512)S(1)}, u32[]{:S(2)}) copy-start(f32[512]{0:T(512)S(1)} %fusion.1) | copy-start | bytes 6148

commit v2 on v0

v2 whole, which is shorter than its diff:
```python
import functools

import jax
import jax.numpy as jnp
import numpy as np
from jax import lax
from jax.experimental import pallas as pl
from jax.experimental.pallas import tpu as pltpu
from jax.sharding import PartitionSpec as P

NPTS = 262144
TILE = 512
AXES = ("oh", "core", "pt")
upper_bound = 8.0
quot_eps = 1e-06


def split3(v):
    hi = v.astype(jnp.bfloat16)
    rest = v - hi.astype(jnp.float32)
    mid = rest.astype(jnp.bfloat16)
    lo = (rest - mid.astype(jnp.float32)).astype(jnp.bfloat16)
    return jnp.concatenate([hi, mid, lo], 1)


def shifted(vs, k):
    return [pltpu.roll(v, k, 1) for v in vs]


def added(xs, ys):
    return [x + y for x, y in zip(xs, ys)]


def filter_kernel(
    first, count, orb_ref, pot_ref, cut_ref, out_ref, abuf, bbuf, wbuf, nat, filt, appl, perm, back, in_sem, out_sem
):
    cut = cut_ref[0]
    center = 0.5 * (upper_bound + cut)
    half_width = 0.5 * (upper_bound - cut)
    alpha = -1.0 / half_width
    odd_lane = (lax.broadcasted_iota(jnp.int32, (8, 128), 1) & 1) == 1
    row = lax.broadcasted_iota(jnp.int32, (256, 256), 0)
    col = lax.broadcasted_iota(jnp.int32, (256, 256), 1)

    def target(k):
        return ((k >> 6) & 1) * 128 + (k & 63) * 2 + (k >> 7)

    for part in range(3):
        perm[256 * part : 256 * part + 256, :] = jnp.where(target(row) == col, 1.0, 0.0).astype(jnp.bfloat16)
        back[256 * part : 256 * part + 256, :] = jnp.where(target(col) == row, 1.0, 0.0).astype(jnp.bfloat16)

    filt16 = filt.reshape(16, 16, 8, 128)
    appl16 = appl.reshape(16, 16, 8, 128)

    def orb_copy(o, s):
        return pltpu.make_async_copy(
            orb_ref.at[s, :, :, first + o, :], nat.at[o % 2, :, :, s, :], in_sem.at[o % 2, s]
        )

    def pot_copy(s):
        return pltpu.make_async_copy(pot_ref.at[s], nat.at[1, :, :, s, :], in_sem.at[1, s])

    def out_copies(o, s):
        return (
            pltpu.make_async_copy(filt16.at[:, :, s, :], out_ref.at[s, :, 2 * o, :, :], out_sem.at[0, s]),
            pltpu.make_async_copy(appl16.at[:, :, s, :], out_ref.at[s, :, 2 * o + 1, :, :], out_sem.at[1, s]),
        )

    def to_blocks(slot, store):
        def body(h, _):
            x0 = 4 * h
            a = nat[slot, pl.ds(x0, 4), :16].reshape(512, 128)
            b = nat[slot, pl.ds(x0, 4), 16:].reshape(512, 128)
            v = jnp.dot(split3(jnp.concatenate([a, b], 1)), perm[...], preferred_element_type=jnp.float32)
            even = v[:, :128].reshape(4, 16, 8, 128)
            odd = v[:, 128:].reshape(4, 16, 8, 128)
            for i in range(4):
                for yp in range(16):
                    store(x0 + i, 2 * yp, even[i, yp])
                    store(x0 + i, 2 * yp + 1, odd[i, yp])
            return 0

        lax.fori_loop(0, 2, body, 0)

    def to_natural(buf, out):
        def body(h, _):
            x0 = 4 * h
            rows = [
                jnp.concatenate([buf[x0 + i, 2 * yp + p] for i in range(4) for yp in range(16)], 0) for p in range(2)
            ]
            v = jnp.dot(split3(jnp.concatenate(rows, 1)), back[...], preferred_element_type=jnp.float32)
            out[pl.ds(x0, 4), :16] = v[:, :128].reshape(4, 16, 8, 128)
            out[pl.ds(x0, 4), 16:] = v[:, 128:].reshape(4, 16, 8, 128)
            return 0

        lax.fori_loop(0, 2, body, 0)

    def flip(v):
        return jnp.where(odd_lane, pltpu.roll(v, 1, 1), pltpu.roll(v, 127, 1))

    def sweep(cur, emit):
        def at(xl):
            return [cur[xl, y] for y in range(32)]

        below = [pltpu.roll(v, 1, 0) for v in at(7)]
        here = at(0)
        wrap = [pltpu.roll(v, 7, 0) for v in here]
        for xl in range(8):
            above = at(xl + 1) if xl < 7 else wrap
            ring = [flip(here[31])] + here + [flip(here[0])]
            zs = added(shifted(here, 2), shifted(here, 126))
            s = added(added(added(below, above), added(ring[:32], ring[2:])), zs)
            emit(xl, here, [alpha * s[y] + wbuf[xl, y] * here[y] for y in range(32)])
            below, here = here, above

    def advance(cur, old):
        def emit(xl, v, t):
            prev = [old[xl, y] for y in range(32)]
            for y in range(32):
                old[xl, y] = t[y] - prev[y]

        sweep(cur, emit)

    for s in range(8):
        pot_copy(s).start()
        orb_copy(0, s).start()
    for s in range(8):
        pot_copy(s).wait()

    def w_store(xl, y, v):
        wbuf[xl, y] = (v + (3.0 - center)) * (2.0 / half_width)

    to_blocks(1, w_store)

    def one(o, _):
        for s in range(8):
            orb_copy(o, s).wait()

        @pl.when(o + 1 < count)
        def _():
            for s in range(8):
                orb_copy(o + 1, s).start()

        def y_store(xl, y, v):
            abuf[xl, y] = v

        to_blocks(o % 2, y_store)

        def emit_first(xl, v, t):
            for y in range(32):
                bbuf[xl, y] = 0.5 * t[y]

        sweep(abuf, emit_first)

        def pair(k, _):
            advance(bbuf, abuf)

            @pl.when(k < 5)
            def _():
                advance(abuf, bbuf)

            return 0

        lax.fori_loop(0, 6, pair, 0)

        @pl.when(o > 0)
        def _():
            for s in range(8):
                for copy in out_copies(o - 1, s):
                    copy.wait()

        def emit_last(xl, v, t):
            for y in range(32):
                bbuf[xl, y] = (0.5 * half_width) * t[y] + center * v[y]

        sweep(abuf, emit_last)
        to_natural(abuf, filt)
        to_natural(bbuf, appl)
        for s in range(8):
            for copy in out_copies(o, s):
                copy.start()
        return 0

    lax.fori_loop(0, count, one, 0)
    for s in range(8):
        for copy in out_copies(count - 1, s):
            copy.wait()


def run_filter(orb, pot, cut, first, count):
    return pl.pallas_call(
        functools.partial(filter_kernel, first, count),
        out_shape=jax.ShapeDtypeStruct((8, 16, 2 * count, 16, 128), jnp.float32),
        in_specs=[
            pl.BlockSpec(memory_space=pl.ANY),
            pl.BlockSpec(memory_space=pl.ANY),
            pl.BlockSpec(memory_space=pltpu.SMEM),
        ],
        out_specs=pl.BlockSpec(memory_space=pl.ANY),
        scratch_shapes=[
            pltpu.VMEM((8, 32, 8, 128), jnp.float32),
            pltpu.VMEM((8, 32, 8, 128), jnp.float32),
            pltpu.VMEM((8, 32, 8, 128), jnp.float32),
            pltpu.VMEM((2, 8, 32, 8, 128), jnp.float32),
            pltpu.VMEM((8, 32, 8, 128), jnp.float32),
            pltpu.VMEM((8, 32, 8, 128), jnp.float32),
            pltpu.VMEM((768, 256), jnp.bfloat16),
            pltpu.VMEM((768, 256), jnp.bfloat16),
            pltpu.SemaphoreType.DMA((2, 8)),
            pltpu.SemaphoreType.DMA((2, 8)),
        ],
        compiler_params=pltpu.CompilerParams(vmem_limit_bytes=60 << 20),
        cost_estimate=pl.CostEstimate(
            flops=count * 13 * NPTS * 2000, bytes_accessed=count << 21, transcendentals=0
        ),
        name="filter",
    )(orb, pot, cut)


def halves(v):
    hi = v.astype(jnp.bfloat16)
    return hi, (v - hi.astype(jnp.float32)).astype(jnp.bfloat16)


def nt(a, b):
    return lax.dot_general(a, b, (((1,), (1,)), ((), ())), preferred_element_type=jnp.float32)


def nn(a, b):
    return jnp.dot(a, b, preferred_element_type=jnp.float32)


def tile_copies(got_ref, xbuf, sems, t):
    copies = []
    for which in range(2):
        for o in range(2):
            for c in range(TILE // 128):
                copies.append(
                    pltpu.make_async_copy(
                        got_ref.at[:, (2 * o + which) * 16 + t * (TILE // 128) + c, :],
                        xbuf.at[t % 2, which, pl.ds(128 * o, 128), pl.ds(128 * c, 128)],
                        sems.at[t % 2, len(copies)],
                    )
                )
    return copies


def load_tile(got_ref, xbuf, sems):
    t = pl.program_id(0)

    @pl.when(t == 0)
    def _():
        for copy in tile_copies(got_ref, xbuf, sems, t):
            copy.start()

    @pl.when(t + 1 < pl.num_programs(0))
    def _():
        for copy in tile_copies(got_ref, xbuf, sems, t + 1):
            copy.start()

    for copy in tile_copies(got_ref, xbuf, sems, t):
        copy.wait()
    return halves(xbuf[t % 2, 0]), halves(xbuf[t % 2, 1])


def split_e(e_ref, e3, first):
    hi, lo = halves(e_ref[:, first : first + 256])
    e3[:, :256] = hi
    e3[:, 256:512] = hi
    e3[:, 512:] = lo


def project_first(got_ref, e_ref, rot_ref, rota_ref, fh_ref, fl_ref, mat_ref, e3, xbuf, sems):
    @pl.when(pl.program_id(0) == 0)
    def _():
        split_e(e_ref, e3, 0)
        mat_ref[...] = jnp.zeros_like(mat_ref)

    (fh, fl), (ah, al) = load_tile(got_ref, xbuf, sems)
    fh_ref[...] = fh
    fl_ref[...] = fl
    rot_ref[...] = nn(e3[...], jnp.concatenate([fh, fl, fh], 0))
    rota_ref[...] = nn(e3[...], jnp.concatenate([ah, al, ah], 0))
    right = jnp.concatenate([jnp.concatenate([fh, fl, fh], 1), jnp.concatenate([ah, al, ah], 1)], 0)
    mat_ref[...] += nt(jnp.concatenate([fh, fh, fl], 1), right)


def project_last(
    got_ref, e_ref, rot0_ref, rota0_ref, f0h_ref, f0l_ref, mat0_ref, core_ref,
    rot_ref, rota_ref, keep_ref, send_ref, e3, xbuf, mat, acc_n, acc_d, sems,
):
    @pl.when(pl.program_id(0) == 0)
    def _():
        split_e(e_ref, e3, 256)
        mat[...] = jnp.zeros_like(mat)
        acc_n[...] = jnp.zeros_like(acc_n)
        acc_d[...] = jnp.zeros_like(acc_d)

    (fh, fl), (ah, al) = load_tile(got_ref, xbuf, sems)
    f0h, f0l = f0h_ref[...], f0l_ref[...]
    left = jnp.concatenate([jnp.concatenate([f0h, f0h, f0l], 1), jnp.concatenate([fh, fh, fl], 1)], 0)
    right = jnp.concatenate([jnp.concatenate([fh, fl, fh], 1), jnp.concatenate([ah, al, ah], 1)], 0)
    mat[...] += nt(left, right)
    rot = rot0_ref[...] + nn(e3[...], jnp.concatenate([fh, fl, fh], 0))
    rota = rota0_ref[...] + nn(e3[...], jnp.concatenate([ah, al, ah], 0))
    rot_ref[...] = rot
    rota_ref[...] = rota
    pn, pd = rot * rota, rot * rot
    acc_n[...] += sum(pn[:, 128 * c : 128 * c + 128] for c in range(TILE // 128))
    acc_d[...] += sum(pd[:, 128 * c : 128 * c + 128] for c in range(TILE // 128))

    @pl.when(pl.program_id(0) == pl.num_programs(0) - 1)
    def _():
        scale = 1.0 / NPTS
        me = core_ref[0]
        rows = []
        for m in range(2):
            here = slice(256 * m, 256 * m + 256)
            upper = mat[:256, here]
            rows.append(jnp.concatenate([mat0_ref[:, here], upper], 1) * scale)
            rows.append(jnp.concatenate([upper.T, mat[256:, here]], 1) * scale)
        sums = []
        for acc in (acc_n, acc_d):
            for q in range(4):
                sums.append(jnp.sum(acc[128 * q : 128 * q + 128, :].T, axis=0, keepdims=True) * scale)

        def put(ref, core):
            for oh in range(8):
                src = oh * 16 + core * 8
                base = oh * 8 * 40
                for m in range(2):
                    for o in range(4):
                        block = rows[2 * m + o // 2]
                        r0 = (o % 2) * 128 + src
                        for q in range(4):
                            ref[pl.ds(base + m * 16 + o * 4 + q, 8, stride=40), :] = block[
                                r0 : r0 + 8, 128 * q : 128 * q + 128
                            ]
                for k in range(8):
                    ref[pl.ds(base + 32 + k, 8, stride=40), :] = jnp.broadcast_to(sums[k], (8, 128))

        for core in range(2):

            @pl.when(me == core)
            def _():
                put(keep_ref, core)
                put(send_ref, 1 - core)


def run_projects(got0, got1, et, core):
    f32, bf16 = jnp.float32, jnp.bfloat16
    steps = 2048 // TILE
    hbm = pl.BlockSpec(memory_space=pl.ANY)
    cols = pl.BlockSpec((512, TILE), lambda t: (0, t))
    fcols = pl.BlockSpec((256, TILE), lambda t: (0, t))

    def whole(*shape):
        return pl.BlockSpec(shape, lambda t: (0,) * len(shape))

    full = jax.ShapeDtypeStruct((512, 2048), f32)
    part = jax.ShapeDtypeStruct((256, 2048), bf16)
    scratch = [pltpu.VMEM((512, 768), bf16), pltpu.VMEM((2, 2, 256, TILE), f32)]
    sems = pltpu.SemaphoreType.DMA((2, 4 * TILE // 128))
    first = pl.pallas_call(
        project_first,
        grid=(steps,),
        out_shape=(full, full, part, part, jax.ShapeDtypeStruct((256, 512), f32)),
        in_specs=[hbm, whole(512, 512)],
        out_specs=(cols, cols, fcols, fcols, whole(256, 512)),
        scratch_shapes=scratch + [sems],
        compiler_params=pltpu.CompilerParams(vmem_limit_bytes=40 << 20),
        cost_estimate=pl.CostEstimate(flops=8 << 30, bytes_accessed=16 << 20, transcendentals=0),
        name="project_first",
    )(got0, et)
    return pl.pallas_call(
        project_last,
        grid=(steps,),
        out_shape=(full, full) + (jax.ShapeDtypeStruct((64 * 40, 128), f32),) * 2,
        in_specs=[hbm, whole(512, 512), cols, cols, fcols, fcols, whole(256, 512), pl.BlockSpec(memory_space=pltpu.SMEM)],
        out_specs=(cols, cols, whole(64 * 40, 128), whole(64 * 40, 128)),
        scratch_shapes=scratch
        + [pltpu.VMEM((512, 512), f32), pltpu.VMEM((512, 128), f32), pltpu.VMEM((512, 128), f32), sems],
        compiler_params=pltpu.CompilerParams(vmem_limit_bytes=40 << 20),
        cost_estimate=pl.CostEstimate(flops=8 << 30, bytes_accessed=24 << 20, transcendentals=0),
        name="project_last",
    )(got1, et, *first, core)


def on_device(orbitals, potential, cutoff, eigvec):
    orb = orbitals.reshape(4, 2048, 128).transpose(1, 0, 2).reshape(8, 8, 32, 4, 128)
    pot = potential.reshape(8, 8, 32, 128)
    et = eigvec.reshape(128, 4, 512).transpose(2, 1, 0).reshape(512, 512)
    got = []
    for first in (0, 2):
        sent = run_filter(orb, pot, cutoff, first, 2).reshape(128, 64, 128)
        got.append(lax.all_to_all(sent, AXES, split_axis=0, concat_axis=0, tiled=True))
    core = lax.axis_index("core").astype(jnp.int32).reshape(1)
    rotated, rot_applied, keep, send = run_projects(got[0], got[1], et, core)
    pay = keep + lax.ppermute(send, "core", [(0, 1), (1, 0)])
    pay = lax.all_to_all(pay.reshape(64, 40, 128), ("oh", "pt"), split_axis=0, concat_axis=0, tiled=True)
    total = jnp.sum(pay, axis=0)
    mats = total[:32].reshape(2, 4, 4, 128).transpose(0, 1, 3, 2).reshape(2, 4, 512)
    numer = total[32:36].reshape(512)
    denom = total[36:40].reshape(512)
    ritz = numer / (denom + quot_eps)
    residual = rot_applied - ritz[:, None] * rotated
    return (mats[0], mats[1], rotated, residual, ritz)


def solution(mesh):
    fine = jax.sharding.Mesh(np.asarray(mesh.devices).reshape(8, 2, 8), AXES)
    return jax.shard_map(
        on_device,
        mesh=fine,
        in_specs=(P(AXES, None), P(), P(), P()),
        out_specs=(P(AXES, None), P(AXES, None), P(None, AXES), P(None, AXES), P()),
        check_vma=False,
    )
```

time: 1020 us -> 204 us (0.20)
  local copies, waits for them, and re-layouts: 348 us -> 10.6 us
  other arithmetic: 299 us -> 6.2 us
  waiting for transfers between devices: 179 us -> 67.6 us
  blocking collectives: 127 us -> 26.8 us
  Pallas kernels: 0 us -> 72.5 us
  matrix products: 40.3 us -> 0 us
  between operations: 15.1 us -> 1.43 us
  starting transfers between devices: 6.25 us -> 18.1 us
    sub x11 -> x1, other arithmetic: 229 us -> 5.95 us  [on_device(): residual = rot_applied - ritz[:, None] * rotated]
    slice x104 -> x4, local copies, waits for them, and re-layouts: 184 us -> 0.29 us  [the longest x3 0.29 us: on_device(): return (mats[0], mats[1], rotated, residual, ritz)]
    unnamed x2 -> x0, waiting for transfers between devices: 132 us -> none
    while x88 -> x0, local copies, waits for them, and re-layouts: 124 us -> none
    pallas_call x0 -> x4, Pallas kernels: none -> 72.5 us  [the longest x2 50.8 us: run_filter(): pl.pallas_call(functools.partial(filter_kernel, first, count), out_shape=...]
    psum x1 -> x0, blocking collectives: 63.8 us -> none  [on_device(): numer, denom = lax.psum((numer, denom), ('ob', 'pt'))]
    dot_general x6 -> x0, matrix products: 40.3 us -> none  [the longest x1 10.6 us: on_device(): rot_applied = jnp.dot(eigvec.T, rows_appl, precision=high)]
    all_to_all x1, blocking collectives: 63.7 us -> 26.8 us  [on_device(): lax.all_to_all(pay.reshape(64, 40, 128), ('oh', 'pt'), split_axis=0, conc...]
  transfers between devices with their start and end apart: 2 -> 3, of which waited for: 2 -> 3; matrix products, arithmetic and copies ran while one was open for 2% -> 0% of each run, Pallas kernels for 0% -> 17%
where the time goes in v2:
time: 204 us; the launch traced here: 203 us
  Pallas kernels  72.5 us (36%)
  waiting for transfers between devices  67.6 us (33%)
  blocking collectives  26.8 us (13%)
  starting transfers between devices  18.1 us (9%)
  local copies, waits for them, and re-layouts  10.6 us (5%)
  other arithmetic  6.2 us (3%)
    all_to_all x2, waiting for transfers between devices, on_device(): lax.all_to_all(sent, AXES, split_axis=0, concat_axis=0, tiled=True)  64.6 us
    pallas_call x2, Pallas kernels, run_filter(): pl.pallas_call(functools.partial(filter_kernel, first, count), out_shape=...  50.8 us
    all_to_all x1, blocking collectives, on_device(): lax.all_to_all(pay.reshape(64, 40, 128), ('oh', 'pt'), split_axis=0, conc...  26.8 us
    all_to_all x2, starting transfers between devices, on_device(): lax.all_to_all(sent, AXES, split_axis=0, concat_axis=0, tiled=True)  18.1 us
    pallas_call x1, Pallas kernels, run_projects(): pl.pallas_call(project_last, grid=(steps,), out_shape=(full, full) + (jax...  13.2 us
    pallas_call x1, Pallas kernels, run_projects(): pl.pallas_call(project_first, grid=(steps,), out_shape=(full, full, part,...  8.45 us
    unnamed x15, local copies, waits for them, and re-layouts  7.83 us
    sub x1, other arithmetic, on_device(): residual = rot_applied - ritz[:, None] * rotated  5.95 us
  transfers between devices with their start and end apart: 3, of which 3 were waited for; matrix products, arithmetic and copies ran while one was open for 0% of the time, Pallas kernels for 17%

profile of v2, /device:TPU:0, one launch (start us, length us, event | category | flops | bytes accessed | tf_op | source)
XLA Modules:
  0.0 203.2 jit_solution(10106156327883075671)
XLA Ops:
  1.3 25.4 %filter.3 = f32[8,16,4,16,128]{4,3,2,1,0:T(8,128)} custom-call(f32[8,8,32,4,128]{4,3,2,1,0:T(4,128)} %bitcast.31, f32[8,8,32,128]{3,2,1,0:T(8,128)} %bitcast.33, f32[1]{0:T(128)S(6)} %copy.18.cut_ref), custom_call_target="tpu_custom_call" | custom-call | flops 13631488000 | bytes 4194304 | tf_op jit(solution)/shard_map/filter/pallas_call | solution.py:191
  26.7 11.7 %all-to-all-start.1 = ((f32[128,64,128]{2,1,0:T(8,128)}), f32[128,64,128]{2,1,0:T(8,128)}, u32[]{:S(2)}, u32[]{:S(2)}) async-start(f32[128,64,128]{2,1,0:T(8,128)} %bitcast.28), calls=%async_computation.1 | async-start | bytes 8388608 | tf_op jit(solution)/shard_map/all_to_all | solution.py:396
  38.4 25.4 %filter.2 = f32[8,16,4,16,128]{4,3,2,1,0:T(8,128)} custom-call(f32[8,8,32,4,128]{4,3,2,1,0:T(4,128)} %bitcast.32, f32[8,8,32,128]{3,2,1,0:T(8,128)} %bitcast.34, f32[1]{0:T(128)S(6)} %copy.18.cut_ref), custom_call_target="tpu_custom_call" | custom-call | flops 13631488000 | bytes 4194304 | tf_op jit(solution)/shard_map/filter/pallas_call | solution.py:191
  63.8 26.8 %all-to-all-done.1.got_ref = f32[128,64,128]{2,1,0:T(8,128)} async-done(((f32[128,64,128]{2,1,0:T(8,128)}), f32[128,64,128]{2,1,0:T(8,128)}, u32[]{:S(2)}, u32[]{:S(2)}) %all-to-all-start.1) | async-done | bytes 4194336 | tf_op jit(solution)/shard_map/all_to_all | solution.py:396
  90.6 0.0 copy-start.5
  90.6 6.4 %all-to-all-start = ((f32[128,64,128]{2,1,0:T(8,128)}), f32[128,64,128]{2,1,0:T(8,128)}, u32[]{:S(2)}, u32[]{:S(2)}) async-start(f32[128,64,128]{2,1,0:T(8,128)} %bitcast.27), calls=%async_computation | async-start | bytes 8388608 | tf_op jit(solution)/shard_map/all_to_all | solution.py:396
  97.0 0.0 copy-done.5
  97.0 0.3 reshape.64
  97.3 0.6 copy.12
  97.9 0.1 copy.17
  98.0 8.5 %project_first.1 = (f32[512,2048]{1,0:T(8,128)S(1)}, f32[512,2048]{1,0:T(8,128)S(1)}, bf16[256,2048]{1,0:T(8,128)(2,1)S(1)}, bf16[256,2048]{1,0:T(8,128)(2,1)S(1)}, f32[256,512]{1,0:T(8,128)S(1)}) custom-call(f32[128,64,128]{2,1,0:T(8,128)} %all-to-all-done.1.got_ref, f32[512,512]{1,0:T(8,128)S(1)} %bitcast.24), custom_call_target="tpu_custom_call" | custom-call | flops 8589934592 | bytes 16777216 | tf_op jit(solution)/shard_map/project_first/pallas_call | solution.py:364
  106.4 0.0 copy-start.1
  106.4 2.0 copy-done.1
  108.4 0.0 copy-start.2
  108.4 2.0 copy-done.2
  110.3 0.8 copy-done.3
  111.1 37.8 %all-to-all-done.got_ref = f32[128,64,128]{2,1,0:T(8,128)} async-done(((f32[128,64,128]{2,1,0:T(8,128)}), f32[128,64,128]{2,1,0:T(8,128)}, u32[]{:S(2)}, u32[]{:S(2)}) %all-to-all-start) | async-done | bytes 4194336 | tf_op jit(solution)/shard_map/all_to_all | solution.py:396
  149.0 1.0 copy-done.4
  150.0 13.2 %project_last.1 = (f32[512,2048]{1,0:T(8,128)}, f32[512,2048]{1,0:T(8,128)S(1)}, f32[2560,128]{1,0:T(8,128)S(1)}, f32[2560,128]{1,0:T(8,128)S(1)}) custom-call(f32[128,64,128]{2,1,0:T(8,128)} %all-to-all-done.got_ref, f32[512,512]{1,0:T(8,128)S(1)} %bitcast.25, f32[512,2048]{1,0:T(8,128)} %copy-done.1, f32[512,2048]{1,0:T(8,128)} %copy-done.2, ...), custom_call_target="tpu_custom_call" | custom-call | flops 8589934592 | bytes 25165824 | tf_op jit(solution)/shard_map/project_last/pallas_call | solution.py:375
  163.2 0.0 copy-start
  163.2 2.0 copy-done
  165.2 0.0 collective-permute-start
  165.2 3.0 %collective-permute-done = f32[2560,128]{1,0:T(8,128)S(1)} collective-permute-done((f32[2560,128]{1,0:T(8,128)S(1)}, f32[2560,128]{1,0:T(8,128)S(1)}, u32[]{:S(2)}, u32[]{:S(2)}) %collective-permute-start) | collective-permute-done | bytes 1310752 | tf_op jit(solution)/shard_map/ppermute | solution.py:399
  168.2 0.1 add.14
  168.4 26.8 %all_to_all.15 = f32[64,40,128]{2,1,0:T(8,128)S(1)} all-to-all(f32[64,40,128]{2,1,0:T(8,128)S(1)} %bitcast.26), channel_id=1, replica_groups=mesh['oh'=8,'core'=2,'pt'=8] {'oh','pt'}, dimensions={0} | all-to-all | bytes 2621440 | tf_op jit(solution)/shard_map/all_to_all | solution.py:400
  195.2 0.1 reduce_sum.9
  195.4 0.1 copy.14
  195.5 0.8 squeeze.7
  196.3 0.1 copy.13
  196.4 0.8 squeeze.6
  197.2 5.9 %multiply_subtract_fusion = f32[512,2048]{1,0:T(8,128)} fusion(f32[512,2048]{1,0:T(8,128)} %copy-done, f32[512,2048]{1,0:T(8,128)} %get-tuple-element.11, f32[512]{0:T(512)S(1)} %fusion.1), kind=kLoop, calls=%fused_computation | loop fusion | flops 2097152 | bytes 12584960 | tf_op jit(solution)/shard_map/sub | solution.py:406
  203.2 0.0 copy-done.6
  (6 shorter events, 0.0 us)
Async XLA Ops:
  26.7 63.9 %all-to-all-start.1 = ((f32[128,64,128]{2,1,0:T(8,128)}), f32[128,64,128]{2,1,0:T(8,128)}, u32[]{:S(2)}, u32[]{:S(2)}) async-start(f32[128,64,128]{2,1,0:T(8,128)} %bitcast.28), calls=%async_computation.1 | async-start | bytes 8388608 | tf_op jit(solution)/shard_map/all_to_all | solution.py:396
  90.6 6.4 %copy-start.5 = (f32[512,512]{1,0:T(8,128)S(1)}, f32[512,512]{1,0:T(8,128)}, u32[]{:S(2)}) copy-start(f32[512,512]{1,0:T(8,128)} %param.7) | copy-start | bytes 3145732
  90.6 58.4 %all-to-all-start = ((f32[128,64,128]{2,1,0:T(8,128)}), f32[128,64,128]{2,1,0:T(8,128)}, u32[]{:S(2)}, u32[]{:S(2)}) async-start(f32[128,64,128]{2,1,0:T(8,128)} %bitcast.27), calls=%async_computation | async-start | bytes 8388608 | tf_op jit(solution)/shard_map/all_to_all | solution.py:396
  106.4 2.0 copy-start.1
  108.4 2.0 copy-start.2
  110.3 0.8 copy-start.3
  149.0 1.0 copy-start.4
  163.2 2.0 copy-start
  165.2 3.0 %collective-permute-start = (f32[2560,128]{1,0:T(8,128)S(1)}, f32[2560,128]{1,0:T(8,128)S(1)}, u32[]{:S(2)}, u32[]{:S(2)}) collective-permute-start(f32[2560,128]{1,0:T(8,128)S(1)} %get-tuple-element.20), channel_id=1, source_target_pairs={{0,8},{8,0},{1,9},{9,1},{2,10},{10,2},{3,11},{11,3},{4,12},{12,4},... | collective-permute-start | bytes 3932168 | tf_op jit(solution)/shard_map/ppermute | solution.py:399
  195.3 7.8 %copy-start.6 = (f32[512]{0:T(512)}, f32[512]{0:T(512)S(1)}, u32[]{:S(2)}) copy-start(f32[512]{0:T(512)S(1)} %fusion.1) | copy-start | bytes 6148

commit v3 on v2

v3 whole, which is shorter than its diff:
```python
import functools

import jax
import jax.numpy as jnp
import numpy as np
from jax import lax
from jax.experimental import pallas as pl
from jax.experimental.pallas import tpu as pltpu
from jax.sharding import PartitionSpec as P

NPTS = 262144
TILE = 512
FINISH = 64
CHUNKS = (2, 2)
AXES = ("oh", "core", "pt")
upper_bound = 8.0
quot_eps = 1e-06


def split3(v):
    hi = v.astype(jnp.bfloat16)
    rest = v - hi.astype(jnp.float32)
    mid = rest.astype(jnp.bfloat16)
    lo = (rest - mid.astype(jnp.float32)).astype(jnp.bfloat16)
    return jnp.concatenate([hi, mid, lo], 1)


def shifted(vs, k):
    return [pltpu.roll(v, k, 1) for v in vs]


def added(xs, ys):
    return [x + y for x, y in zip(xs, ys)]


def filter_kernel(
    first, count, orb_ref, pot_ref, cut_ref, out_ref, abuf, bbuf, wbuf, nat, filt, appl, perm, back, in_sem, out_sem
):
    cut = cut_ref[0]
    center = 0.5 * (upper_bound + cut)
    half_width = 0.5 * (upper_bound - cut)
    alpha = -1.0 / half_width
    odd_lane = (lax.broadcasted_iota(jnp.int32, (8, 128), 1) & 1) == 1
    row = lax.broadcasted_iota(jnp.int32, (256, 256), 0)
    col = lax.broadcasted_iota(jnp.int32, (256, 256), 1)

    def target(k):
        return ((k >> 6) & 1) * 128 + (k & 63) * 2 + (k >> 7)

    for part in range(3):
        perm[256 * part : 256 * part + 256, :] = jnp.where(target(row) == col, 1.0, 0.0).astype(jnp.bfloat16)
        back[256 * part : 256 * part + 256, :] = jnp.where(target(col) == row, 1.0, 0.0).astype(jnp.bfloat16)

    filt16 = filt.reshape(16, 16, 8, 128)
    appl16 = appl.reshape(16, 16, 8, 128)

    def orb_copy(o, s):
        return pltpu.make_async_copy(
            orb_ref.at[s, :, :, first + o, :], nat.at[o % 2, :, :, s, :], in_sem.at[o % 2, s]
        )

    def pot_copy(s):
        return pltpu.make_async_copy(pot_ref.at[s], nat.at[1, :, :, s, :], in_sem.at[1, s])

    def out_copy(o, which, s):
        src = (filt16, appl16)[which].at[:, :, s, :]
        return pltpu.make_async_copy(src, out_ref.at[s, :, 2 * o + which, :, :], out_sem.at[which, s])

    def to_blocks(slot, store):
        def body(h, _):
            x0 = 4 * h
            a = nat[slot, pl.ds(x0, 4), :16].reshape(512, 128)
            b = nat[slot, pl.ds(x0, 4), 16:].reshape(512, 128)
            v = jnp.dot(split3(jnp.concatenate([a, b], 1)), perm[...], preferred_element_type=jnp.float32)
            even = v[:, :128].reshape(4, 16, 8, 128)
            odd = v[:, 128:].reshape(4, 16, 8, 128)
            for i in range(4):
                for yp in range(16):
                    store(x0 + i, 2 * yp, even[i, yp])
                    store(x0 + i, 2 * yp + 1, odd[i, yp])
            return 0

        lax.fori_loop(0, 2, body, 0)

    def to_natural(buf, out):
        def body(h, _):
            x0 = 4 * h
            rows = [
                jnp.concatenate([buf[x0 + i, 2 * yp + p] for i in range(4) for yp in range(16)], 0) for p in range(2)
            ]
            v = jnp.dot(split3(jnp.concatenate(rows, 1)), back[...], preferred_element_type=jnp.float32)
            out[pl.ds(x0, 4), :16] = v[:, :128].reshape(4, 16, 8, 128)
            out[pl.ds(x0, 4), 16:] = v[:, 128:].reshape(4, 16, 8, 128)
            return 0

        lax.fori_loop(0, 2, body, 0)

    def flip(v):
        return jnp.where(odd_lane, pltpu.roll(v, 1, 1), pltpu.roll(v, 127, 1))

    def sweep(cur, emit):
        def at(xl):
            return [cur[xl, y] for y in range(32)]

        below = [pltpu.roll(v, 1, 0) for v in at(7)]
        here = at(0)
        wrap = [pltpu.roll(v, 7, 0) for v in here]
        for xl in range(8):
            above = at(xl + 1) if xl < 7 else wrap
            ring = [flip(here[31])] + here + [flip(here[0])]
            zs = added(shifted(here, 2), shifted(here, 126))
            s = added(added(added(below, above), added(ring[:32], ring[2:])), zs)
            emit(xl, here, [alpha * s[y] + wbuf[xl, y] * here[y] for y in range(32)])
            below, here = here, above

    def advance(cur, old):
        def emit(xl, v, t):
            prev = [old[xl, y] for y in range(32)]
            for y in range(32):
                old[xl, y] = t[y] - prev[y]

        sweep(cur, emit)

    for s in range(8):
        pot_copy(s).start()
        orb_copy(0, s).start()
    for s in range(8):
        pot_copy(s).wait()

    def w_store(xl, y, v):
        wbuf[xl, y] = (v + (3.0 - center)) * (2.0 / half_width)

    to_blocks(1, w_store)

    def one(o, _):
        for s in range(8):
            orb_copy(o, s).wait()

        @pl.when(o + 1 < count)
        def _():
            for s in range(8):
                orb_copy(o + 1, s).start()

        def y_store(xl, y, v):
            abuf[xl, y] = v

        to_blocks(o % 2, y_store)

        def emit_first(xl, v, t):
            for y in range(32):
                bbuf[xl, y] = 0.5 * t[y]

        sweep(abuf, emit_first)

        def pair(k, _):
            advance(bbuf, abuf)

            @pl.when(k < 5)
            def _():
                advance(abuf, bbuf)

            return 0

        lax.fori_loop(0, 6, pair, 0)

        @pl.when(o > 0)
        def _():
            for s in range(8):
                out_copy(o - 1, 0, s).wait()
                out_copy(o - 1, 1, s).wait()

        def emit_last(xl, v, t):
            for y in range(32):
                bbuf[xl, y] = (0.5 * half_width) * t[y] + center * v[y]

        to_natural(abuf, filt)
        for s in range(8):
            out_copy(o, 0, s).start()
        sweep(abuf, emit_last)
        to_natural(bbuf, appl)
        for s in range(8):
            out_copy(o, 1, s).start()
        return 0

    lax.fori_loop(0, count, one, 0)
    for s in range(8):
        out_copy(count - 1, 0, s).wait()
        out_copy(count - 1, 1, s).wait()


def run_filter(orb, pot, cut, first, count):
    return pl.pallas_call(
        functools.partial(filter_kernel, first, count),
        out_shape=jax.ShapeDtypeStruct((8, 16, 2 * count, 16, 128), jnp.float32),
        in_specs=[
            pl.BlockSpec(memory_space=pl.ANY),
            pl.BlockSpec(memory_space=pl.ANY),
            pl.BlockSpec(memory_space=pltpu.SMEM),
        ],
        out_specs=pl.BlockSpec(memory_space=pl.ANY),
        scratch_shapes=[
            pltpu.VMEM((8, 32, 8, 128), jnp.float32),
            pltpu.VMEM((8, 32, 8, 128), jnp.float32),
            pltpu.VMEM((8, 32, 8, 128), jnp.float32),
            pltpu.VMEM((2, 8, 32, 8, 128), jnp.float32),
            pltpu.VMEM((8, 32, 8, 128), jnp.float32),
            pltpu.VMEM((8, 32, 8, 128), jnp.float32),
            pltpu.VMEM((768, 256), jnp.bfloat16),
            pltpu.VMEM((768, 256), jnp.bfloat16),
            pltpu.SemaphoreType.DMA((2, 8)),
            pltpu.SemaphoreType.DMA((2, 8)),
        ],
        compiler_params=pltpu.CompilerParams(vmem_limit_bytes=60 << 20),
        cost_estimate=pl.CostEstimate(
            flops=count * 13 * NPTS * 2000, bytes_accessed=count << 21, transcendentals=0
        ),
        name="filter",
    )(orb, pot, cut)


def halves(v):
    hi = v.astype(jnp.bfloat16)
    return hi, (v - hi.astype(jnp.float32)).astype(jnp.bfloat16)


def nt(a, b):
    return lax.dot_general(a, b, (((1,), (1,)), ((), ())), preferred_element_type=jnp.float32)


def nn(a, b):
    return jnp.dot(a, b, preferred_element_type=jnp.float32)


def tile_copies(got_refs, counts, xbuf, sems, t):
    copies = []
    for which in range(2):
        row = 0
        for got_ref, count in zip(got_refs, counts):
            for o in range(count):
                for c in range(TILE // 128):
                    copies.append(
                        pltpu.make_async_copy(
                            got_ref.at[:, (2 * o + which) * 16 + t * (TILE // 128) + c, :],
                            xbuf.at[t % 2, which, pl.ds(row, 128), pl.ds(128 * c, 128)],
                            sems.at[t % 2, len(copies)],
                        )
                    )
                row += 128
    return copies


def load_tile(got_refs, counts, xbuf, sems):
    t = pl.program_id(0)

    @pl.when(t == 0)
    def _():
        for copy in tile_copies(got_refs, counts, xbuf, sems, t):
            copy.start()

    @pl.when(t + 1 < pl.num_programs(0))
    def _():
        for copy in tile_copies(got_refs, counts, xbuf, sems, t + 1):
            copy.start()

    for copy in tile_copies(got_refs, counts, xbuf, sems, t):
        copy.wait()
    return halves(xbuf[t % 2, 0]), halves(xbuf[t % 2, 1])


def in_hbm(*arrays):
    return [pltpu.with_memory_space_constraint(x, pltpu.HBM) for x in arrays]


def beside(parts, axis):
    return parts[0] if len(parts) == 1 else jnp.concatenate(parts, axis)


def full_rows(mats, m, i):
    starts = [128 * sum(CHUNKS[:k]) for k in range(len(CHUNKS) + 1)]

    def upper(i, k):
        width = 128 * CHUNKS[k]
        return mats[k][starts[i] : starts[i + 1], m * width : (m + 1) * width]

    return jnp.concatenate([upper(i, k) if k >= i else upper(k, i).T for k in range(len(CHUNKS))], 1)


def overlap_kernel(k, *refs):
    refs = list(refs)

    def take(n):
        out, refs[:] = refs[:n], refs[n:]
        return out

    count, last = CHUNKS[k], k == len(CHUNKS) - 1
    got_ref, *before = take(1 + 2 * k)
    if last:
        mats0 = take(k)
        e_ref, core_ref, keep_ref, send_ref, mat = take(5)
    else:
        fh_ref, fl_ref, mat = take(3)
    xbuf, sems = take(2)

    @pl.when(pl.program_id(0) == 0)
    def _():
        mat[...] = jnp.zeros_like(mat)

    (fh, fl), (ah, al) = load_tile([got_ref], [count], xbuf, sems)
    rows = [(before[2 * i][...], before[2 * i + 1][...]) for i in range(k)] + [(fh, fl)]
    left = beside([jnp.concatenate([h, h, l], 1) for h, l in rows], 0)
    right = jnp.concatenate([jnp.concatenate([fh, fl, fh], 1), jnp.concatenate([ah, al, ah], 1)], 0)
    mat[...] += nt(left, right)
    if not last:
        fh_ref[...] = fh
        fl_ref[...] = fl
        return

    @pl.when(pl.program_id(0) == pl.num_programs(0) - 1)
    def _():
        me = core_ref[0]
        mats = [ref[...] * (1.0 / NPTS) for ref in mats0] + [mat[...] * (1.0 / NPTS)]
        blocks = [[full_rows(mats, m, i) for i in range(len(CHUNKS))] for m in range(2)]
        where = [(i, o) for i in range(len(CHUNKS)) for o in range(CHUNKS[i])]
        e = e_ref[...]
        eh, el = halves(e)
        e3 = jnp.concatenate([eh, eh, el], 1)
        sums = []
        for m in (1, 0):
            h, l = halves(jnp.concatenate(blocks[m], 0))
            p = nn(e3, jnp.concatenate([h, l, h], 0)) * e
            acc = (p[:, :128] + p[:, 128:256]) + (p[:, 256:384] + p[:, 384:])
            for q in range(4):
                sums.append(jnp.sum(acc[128 * q : 128 * q + 128, :].T, axis=0, keepdims=True))
        sums = jnp.concatenate(sums, 0)

        def put(ref, core):
            for oh in range(8):
                base = oh * 8 * 40
                for m in range(2):
                    for o in range(4):
                        i, inner = where[o]
                        r0 = inner * 128 + oh * 16 + core * 8
                        for q in range(4):
                            ref[pl.ds(base + m * 16 + o * 4 + q, 8, stride=40), :] = blocks[m][i][
                                r0 : r0 + 8, 128 * q : 128 * q + 128
                            ]
                for pt in range(8):
                    ref[pl.ds(base + pt * 40 + 32, 8), :] = sums

        for core in range(2):

            @pl.when(me == core)
            def _():
                put(keep_ref, core)
                put(send_ref, 1 - core)


def cols(n):
    return pl.BlockSpec((n, TILE), lambda t: (0, t))


def whole(*shape):
    return pl.BlockSpec(shape, lambda t: (0,) * len(shape))


def run_overlap(k, got, before, mats, et, core):
    f32, bf16 = jnp.float32, jnp.bfloat16
    count, last = CHUNKS[k], k == len(CHUNKS) - 1
    mat_shape = (128 * sum(CHUNKS[: k + 1]), 256 * count)
    in_specs, args = [pl.BlockSpec(memory_space=pl.ANY)], [got]
    for i in range(k):
        in_specs += [cols(128 * CHUNKS[i])] * 2
        args += list(before[i])
    scratch = [
        pltpu.VMEM((2, 2, 128 * count, TILE), f32),
        pltpu.SemaphoreType.DMA((2, 2 * count * TILE // 128)),
    ]
    if last:
        in_specs += [whole(*m.shape) for m in mats] + [whole(512, 512), pl.BlockSpec(memory_space=pltpu.SMEM)]
        args = in_hbm(*args, *mats, et) + [core]
        out_shape = [jax.ShapeDtypeStruct((64 * 40, 128), f32)] * 2
        out_specs = [whole(64 * 40, 128)] * 2
        scratch = [pltpu.VMEM(mat_shape, f32)] + scratch
    else:
        out_shape = [jax.ShapeDtypeStruct((128 * count, 2048), bf16)] * 2 + [jax.ShapeDtypeStruct(mat_shape, f32)]
        out_specs = [cols(128 * count)] * 2 + [whole(*mat_shape)]
    return pl.pallas_call(
        functools.partial(overlap_kernel, k),
        grid=(2048 // TILE,),
        out_shape=out_shape,
        in_specs=in_specs,
        out_specs=out_specs,
        scratch_shapes=scratch,
        compiler_params=pltpu.CompilerParams(vmem_limit_bytes=(30 if last else 60) << 20),
        cost_estimate=pl.CostEstimate(flops=8 << 30, bytes_accessed=8 << 20, transcendentals=0),
        name="overlap",
    )(*args)


def rotate_kernel(*refs):
    n = len(CHUNKS)
    e_ref, rot_ref, rota_ref, e3, xbuf, sems = refs[n:]

    @pl.when(pl.program_id(0) == 0)
    def _():
        hi, lo = halves(e_ref[...])
        e3[:, :512] = hi
        e3[:, 512:1024] = hi
        e3[:, 1024:] = lo

    (fh, fl), (ah, al) = load_tile(refs[:n], CHUNKS, xbuf, sems)
    rot_ref[...] = nn(e3[...], jnp.concatenate([fh, fl, fh], 0))
    rota_ref[...] = nn(e3[...], jnp.concatenate([ah, al, ah], 0))


def run_rotate(got, et):
    f32 = jnp.float32
    return pl.pallas_call(
        rotate_kernel,
        grid=(2048 // TILE,),
        out_shape=[jax.ShapeDtypeStruct((512, 2048), f32)] * 2,
        in_specs=[pl.BlockSpec(memory_space=pl.ANY)] * len(got) + [whole(512, 512)],
        out_specs=[cols(512)] * 2,
        scratch_shapes=[
            pltpu.VMEM((512, 1536), jnp.bfloat16),
            pltpu.VMEM((2, 2, 512, TILE), f32),
            pltpu.SemaphoreType.DMA((2, 8 * TILE // 128)),
        ],
        compiler_params=pltpu.CompilerParams(vmem_limit_bytes=60 << 20),
        cost_estimate=pl.CostEstimate(flops=16 << 30, bytes_accessed=16 << 20, transcendentals=0),
        name="rotate",
    )(*got, et)


def finish_kernel(pay_ref, rot_ref, rota_ref, gram_ref, ham_ref, ritz_ref, res_ref, tot, scale):
    @pl.when(pl.program_id(0) == 0)
    def _():
        tot[...] = jnp.sum(pay_ref[...], axis=0)
        ritz = tot[32:36, :] / (tot[36:40, :] + quot_eps)
        ritz_ref[...] = ritz
        turned = jnp.concatenate([ritz, ritz], 0).T
        for q in range(4):
            scale[128 * q : 128 * q + 128, :] = jnp.broadcast_to(turned[:, q : q + 1], (128, 128))

    ritz = scale[pl.ds(pl.multiple_of(pl.program_id(0) * FINISH, FINISH), FINISH), :]
    for c in range(2048 // 128):
        at = slice(128 * c, 128 * c + 128)
        res_ref[:, at] = rota_ref[:, at] - ritz * rot_ref[:, at]

    @pl.when(pl.program_id(0) == pl.num_programs(0) - 1)
    def _():
        row = lax.broadcasted_iota(jnp.int32, (512, 512), 0)
        col = lax.broadcasted_iota(jnp.int32, (512, 512), 1)
        perm = jnp.where(4 * (row & 127) + (row >> 7) == col, 1.0, 0.0).astype(jnp.bfloat16)
        parts = split3(jnp.concatenate([tot[pl.ds(q, 8, stride=4), :] for q in range(4)], 1))
        mats = (nn(parts[:, :512], perm) + nn(parts[:, 512:1024], perm)) + nn(parts[:, 1024:], perm)
        gram_ref[...] = mats[:4]
        ham_ref[...] = mats[4:]


def run_finish(pay, rot, rota):
    f32 = jnp.float32
    block = pl.BlockSpec((FINISH, 2048), lambda t: (t, 0))
    return pl.pallas_call(
        finish_kernel,
        grid=(512 // FINISH,),
        out_shape=(
            jax.ShapeDtypeStruct((4, 512), f32),
            jax.ShapeDtypeStruct((4, 512), f32),
            jax.ShapeDtypeStruct((4, 128), f32),
            jax.ShapeDtypeStruct((512, 2048), f32),
        ),
        in_specs=[whole(64, 40, 128), block, block],
        out_specs=(whole(4, 512), whole(4, 512), whole(4, 128), block),
        scratch_shapes=[pltpu.VMEM((40, 128), f32), pltpu.VMEM((512, 128), f32)],
        compiler_params=pltpu.CompilerParams(vmem_limit_bytes=24 << 20),
        cost_estimate=pl.CostEstimate(flops=8 << 20, bytes_accessed=16 << 20, transcendentals=0),
        name="finish",
    )(pay, *in_hbm(rot, rota))


def on_device(orbitals, potential, cutoff, eigvec):
    orb = orbitals.reshape(4, 2048, 128).transpose(1, 0, 2).reshape(8, 8, 32, 4, 128)
    pot = potential.reshape(8, 8, 32, 128)
    et = eigvec.reshape(128, 4, 512).transpose(2, 1, 0).reshape(512, 512)
    core = lax.axis_index("core").astype(jnp.int32).reshape(1)
    gots, before, mats = [], [], []
    for k, count in enumerate(CHUNKS):
        sent = run_filter(orb, pot, cutoff, sum(CHUNKS[:k]), count).reshape(128, 32 * count, 128)
        gots.append(lax.all_to_all(sent, AXES, split_axis=0, concat_axis=0, tiled=True))
        out = run_overlap(k, gots[k], before, mats, et, core)
        if k < len(CHUNKS) - 1:
            before.append(out[:2])
            mats.append(out[2])
    keep, send = out
    pay = (keep + lax.ppermute(send, "core", [(0, 1), (1, 0)])).reshape(64, 40, 128)
    pay, gots[-1] = lax.optimization_barrier((pay, gots[-1]))
    pay = lax.all_to_all(pay, ("oh", "pt"), split_axis=0, concat_axis=0, tiled=True)
    rotated, rot_applied = run_rotate(gots, et)
    gram, hamil_sub, ritz, residual = run_finish(pay, rotated, rot_applied)
    return (gram, hamil_sub, rotated, residual, ritz.reshape(512))


def solution(mesh):
    fine = jax.sharding.Mesh(np.asarray(mesh.devices).reshape(8, 2, 8), AXES)
    return jax.shard_map(
        on_device,
        mesh=fine,
        in_specs=(P(AXES, None), P(), P(), P()),
        out_specs=(P(AXES, None), P(AXES, None), P(None, AXES), P(None, AXES), P()),
        check_vma=False,
    )
```

time: 204 us -> 199 us (0.975)
  blocking collectives: 26.8 us -> 0 us
  Pallas kernels: 72.5 us -> 87.4 us
  waiting for transfers between devices: 67.6 us -> 82.1 us
  local copies, waits for them, and re-layouts: 10.6 us -> 2.01 us
  starting transfers between devices: 18.1 us -> 24.2 us
  other arithmetic: 6.2 us -> 1.19 us
    all_to_all x1 -> x0, blocking collectives: 26.8 us -> none  [on_device(): lax.all_to_all(pay.reshape(64, 40, 128), ('oh', 'pt'), split_axis=0, conc...]
    pallas_call x2 -> x4, Pallas kernels: 21.6 us -> 37.3 us  [the longest x2 16.1 us: run_overlap(): pl.pallas_call(functools.partial(overlap_kernel, k), grid=(2048 // TILE,)...]
    all_to_all x0 -> x1, waiting for transfers between devices: none -> 8.04 us  [on_device(): lax.all_to_all(pay, ('oh', 'pt'), split_axis=0, concat_axis=0, tiled=True)]
    unnamed x15 -> x3, local copies, waits for them, and re-layouts: 7.83 us -> 1.12 us
    all_to_all x2, waiting for transfers between devices: 64.6 us -> 71 us  [on_device(): lax.all_to_all(sent, AXES, split_axis=0, concat_axis=0, tiled=True)]
    all_to_all x0 -> x1, starting transfers between devices: none -> 6.03 us  [on_device(): lax.all_to_all(pay, ('oh', 'pt'), split_axis=0, concat_axis=0, tiled=True)]
    sub x1 -> x0, other arithmetic: 5.95 us -> none  [on_device(): residual = rot_applied - ritz[:, None] * rotated]
  transfers between devices with their start and end apart: 3 -> 4, of which waited for: 3 -> 4; matrix products, arithmetic and copies ran while one was open for 0% -> 1% of each run, Pallas kernels for 17% -> 22%
where the time goes in v3:
time: 199 us; the launch traced here: 198 us
  Pallas kernels  87.4 us (44%)
  waiting for transfers between devices  82.1 us (41%)
  starting transfers between devices  24.2 us (12%)
  local copies, waits for them, and re-layouts  2.01 us (1%)
    all_to_all x2, waiting for transfers between devices, on_device(): lax.all_to_all(sent, AXES, split_axis=0, concat_axis=0, tiled=True)  71 us
    pallas_call x2, Pallas kernels, run_filter(): pl.pallas_call(functools.partial(filter_kernel, first, count), out_shape=...  50.2 us
    all_to_all x2, starting transfers between devices, on_device(): lax.all_to_all(sent, AXES, split_axis=0, concat_axis=0, tiled=True)  18.1 us
    pallas_call x2, Pallas kernels, run_overlap(): pl.pallas_call(functools.partial(overlap_kernel, k), grid=(2048 // TILE,)...  16.1 us
    pallas_call x1, Pallas kernels, run_rotate(): pl.pallas_call(rotate_kernel, grid=(2048 // TILE,), out_shape=[jax.ShapeD...  12.9 us
    pallas_call x1, Pallas kernels, run_finish(): pl.pallas_call(finish_kernel, grid=(512 // FINISH,), out_shape=(jax.Shape...  8.22 us
    all_to_all x1, waiting for transfers between devices, on_device(): lax.all_to_all(pay, ('oh', 'pt'), split_axis=0, concat_axis=0, tiled=True)  8.04 us
    all_to_all x1, starting transfers between devices, on_device(): lax.all_to_all(pay, ('oh', 'pt'), split_axis=0, concat_axis=0, tiled=True)  6.03 us
  transfers between devices with their start and end apart: 4, of which 4 were waited for; matrix products, arithmetic and copies ran while one was open for 1% of the time, Pallas kernels for 22%

profile of v3, /device:TPU:0, one launch (start us, length us, event | category | flops | bytes accessed | tf_op | source)
XLA Modules:
  0.0 198.3 jit_solution(7236794373869562000)
XLA Ops:
  1.3 25.1 %filter.3 = f32[8,16,4,16,128]{4,3,2,1,0:T(8,128)} custom-call(f32[8,8,32,4,128]{4,3,2,1,0:T(4,128)} %bitcast.21, f32[8,8,32,128]{3,2,1,0:T(8,128)} %bitcast.23, f32[1]{0:T(128)S(6)} %copy.14.cut_ref), custom_call_target="tpu_custom_call" | custom-call | flops 13631488000 | bytes 4194304 | tf_op jit(solution)/shard_map/filter/pallas_call | solution.py:192
  26.4 11.7 %all-to-all-start.1 = ((f32[128,64,128]{2,1,0:T(8,128)}), f32[128,64,128]{2,1,0:T(8,128)}, u32[]{:S(2)}, u32[]{:S(2)}) async-start(f32[128,64,128]{2,1,0:T(8,128)} %bitcast.17), calls=%async_computation.1 | async-start | bytes 8388608 | tf_op jit(solution)/shard_map/all_to_all | solution.py:490
  38.1 25.1 %filter.2 = f32[8,16,4,16,128]{4,3,2,1,0:T(8,128)} custom-call(f32[8,8,32,4,128]{4,3,2,1,0:T(4,128)} %bitcast.22, f32[8,8,32,128]{3,2,1,0:T(8,128)} %bitcast.24, f32[1]{0:T(128)S(6)} %copy.14.cut_ref), custom_call_target="tpu_custom_call" | custom-call | flops 13631488000 | bytes 4194304 | tf_op jit(solution)/shard_map/filter/pallas_call | solution.py:192
  63.2 27.1 %all-to-all-done.1.refs_0_ = f32[128,64,128]{2,1,0:T(8,128)} async-done(((f32[128,64,128]{2,1,0:T(8,128)}), f32[128,64,128]{2,1,0:T(8,128)}, u32[]{:S(2)}, u32[]{:S(2)}) %all-to-all-start.1) | async-done | bytes 4194336 | tf_op jit(solution)/shard_map/all_to_all | solution.py:490
  90.2 0.0 copy-start
  90.2 6.4 %all-to-all-start = ((f32[128,64,128]{2,1,0:T(8,128)}), f32[128,64,128]{2,1,0:T(8,128)}, u32[]{:S(2)}, u32[]{:S(2)}) async-start(f32[128,64,128]{2,1,0:T(8,128)} %bitcast.16), calls=%async_computation | async-start | bytes 8388608 | tf_op jit(solution)/shard_map/all_to_all | solution.py:490
  96.6 0.0 copy-done
  96.7 0.3 reshape.45
  97.0 0.6 copy.10
  97.6 1.1 copy.13
  98.7 6.0 %overlap.2 = (bf16[256,2048]{1,0:T(8,128)(2,1)}, bf16[256,2048]{1,0:T(8,128)(2,1)}, f32[256,512]{1,0:T(8,128)}) custom-call(f32[128,64,128]{2,1,0:T(8,128)} %all-to-all-done.1.refs_0_), custom_call_target="tpu_custom_call" | custom-call | flops 8589934592 | bytes 8388608 | tf_op jit(solution)/shard_map/overlap/pallas_call | solution.py:387
  104.7 43.9 %all-to-all-done.refs_0_.refs_1_ = f32[128,64,128]{2,1,0:T(8,128)} async-done(((f32[128,64,128]{2,1,0:T(8,128)}), f32[128,64,128]{2,1,0:T(8,128)}, u32[]{:S(2)}, u32[]{:S(2)}) %all-to-all-start) | async-done | bytes 4194336 | tf_op jit(solution)/shard_map/all_to_all | solution.py:490
  148.6 10.1 %overlap.3 = (f32[2560,128]{1,0:T(8,128)S(1)}, f32[2560,128]{1,0:T(8,128)S(1)}) custom-call(f32[128,64,128]{2,1,0:T(8,128)} %all-to-all-done.refs_0_.refs_1_, bf16[256,2048]{1,0:T(8,128)(2,1)} %get-tuple-element.18.refs_1_, bf16[256,2048]{1,0:T(8,128)(2,1)} %get-tuple-element.19.refs_2_, f32[256,512]{1,0:T(8,128)} %get-tuple-element.20.refs_3_, ...), custom_call_target="tpu_custom_call" | custom-call | flops 8589934592 | bytes 8388608 | tf_op jit(solution)/shard_map/overlap/pallas_call | solution.py:387
  158.7 0.1 collective-permute-start
  158.8 3.0 %collective-permute-done = f32[2560,128]{1,0:T(8,128)S(1)} collective-permute-done((f32[2560,128]{1,0:T(8,128)S(1)}, f32[2560,128]{1,0:T(8,128)S(1)}, u32[]{:S(2)}, u32[]{:S(2)}) %collective-permute-start) | collective-permute-done | bytes 1310752 | tf_op jit(solution)/shard_map/ppermute | solution.py:496
  161.9 1.2 add.3
  163.1 6.0 %all-to-all-start.2 = ((f32[64,40,128]{2,1,0:T(8,128)}), f32[64,40,128]{2,1,0:T(8,128)S(1)}, u32[]{:S(2)}, u32[]{:S(2)}) async-start(f32[64,40,128]{2,1,0:T(8,128)} %bitcast.10), calls=%async_computation.2 | async-start | bytes 2621440 | tf_op jit(solution)/shard_map/all_to_all | solution.py:498
  169.1 12.9 %rotate.1 = (f32[512,2048]{1,0:T(8,128)}, f32[512,2048]{1,0:T(8,128)}) custom-call(f32[128,64,128]{2,1,0:T(8,128)} %all-to-all-done.1.refs_0_, f32[128,64,128]{2,1,0:T(8,128)} %all-to-all-done.refs_0_.refs_1_, f32[512,512]{1,0:T(8,128)} %bitcast.20), custom_call_target="tpu_custom_call" | custom-call | flops 17179869184 | bytes 16777216 | tf_op jit(solution)/shard_map/rotate/pallas_call | solution.py:418
  182.0 8.0 %all-to-all-done.2.pay_ref = f32[64,40,128]{2,1,0:T(8,128)S(1)} async-done(((f32[64,40,128]{2,1,0:T(8,128)}), f32[64,40,128]{2,1,0:T(8,128)S(1)}, u32[]{:S(2)}, u32[]{:S(2)}) %all-to-all-start.2) | async-done | bytes 1310752 | tf_op jit(solution)/shard_map/all_to_all | solution.py:498
  190.1 8.2 %finish.1 = (f32[4,512]{1,0:T(4,128)}, f32[4,512]{1,0:T(4,128)}, f32[4,128]{1,0:T(4,128)}, f32[512,2048]{1,0:T(8,128)}) custom-call(f32[64,40,128]{2,1,0:T(8,128)S(1)} %all-to-all-done.2.pay_ref, f32[512,2048]{1,0:T(8,128)} %get-tuple-element.15.rot_ref, f32[512,2048]{1,0:T(8,128)} %get-tuple-element.26.rota_ref), custom_call_target="tpu_custom_call" | custom-call | flops 8388608 | bytes 16777216 | tf_op jit(solution)/shard_map/finish/pallas_call | solution.py:464
Async XLA Ops:
  26.4 63.9 %all-to-all-start.1 = ((f32[128,64,128]{2,1,0:T(8,128)}), f32[128,64,128]{2,1,0:T(8,128)}, u32[]{:S(2)}, u32[]{:S(2)}) async-start(f32[128,64,128]{2,1,0:T(8,128)} %bitcast.17), calls=%async_computation.1 | async-start | bytes 8388608 | tf_op jit(solution)/shard_map/all_to_all | solution.py:490
  90.2 6.4 %copy-start = (f32[512,512]{1,0:T(8,128)S(1)}, f32[512,512]{1,0:T(8,128)}, u32[]{:S(2)}) copy-start(f32[512,512]{1,0:T(8,128)} %param.7) | copy-start | bytes 3145732
  90.2 58.4 %all-to-all-start = ((f32[128,64,128]{2,1,0:T(8,128)}), f32[128,64,128]{2,1,0:T(8,128)}, u32[]{:S(2)}, u32[]{:S(2)}) async-start(f32[128,64,128]{2,1,0:T(8,128)} %bitcast.16), calls=%async_computation | async-start | bytes 8388608 | tf_op jit(solution)/shard_map/all_to_all | solution.py:490
  158.7 3.1 %collective-permute-start = (f32[2560,128]{1,0:T(8,128)S(1)}, f32[2560,128]{1,0:T(8,128)S(1)}, u32[]{:S(2)}, u32[]{:S(2)}) collective-permute-start(f32[2560,128]{1,0:T(8,128)S(1)} %get-tuple-element.22), channel_id=1, source_target_pairs={{0,8},{8,0},{1,9},{9,1},{2,10},{10,2},{3,11},{11,3},{4,12},{12,4},... | collective-permute-start | bytes 3932168 | tf_op jit(solution)/shard_map/ppermute | solution.py:496
  163.1 27.0 %all-to-all-start.2 = ((f32[64,40,128]{2,1,0:T(8,128)}), f32[64,40,128]{2,1,0:T(8,128)S(1)}, u32[]{:S(2)}, u32[]{:S(2)}) async-start(f32[64,40,128]{2,1,0:T(8,128)} %bitcast.10), calls=%async_computation.2 | async-start | bytes 2621440 | tf_op jit(solution)/shard_map/all_to_all | solution.py:498
